TPU v7x, 128 devices: a whole 4x4x4 slice. The times are simulated.
128 devices in a mesh: row: 8 (over z, core), col: 16 (over y, x).
Axes of the slice: x: 4, y: 4, z: 4, core: 2. Of those that a mesh axis runs over, the one named last changes fastest.
Arguments:
- stored_blocks: float32 [8, 16, 2, 14, 256, 256], P('row', 'col'), may hold values from -0.0390625 to 0.0390625
- onsite: float32 [8, 16, 2, 256], P('row', 'col'), may hold values from 0.05 to 0.95
- bond_mask: int32 [8, 16, 2, 13], P('row', 'col'), may hold values 0 or 1
Outputs:
- purified: float32 [8, 16, 2, 14, 256, 256], P('row', 'col')
All inputs are finite; a program needn't handle non-finite values. No bound on the sum of `bond_mask` on one device may be relied on, other than what follows from the above.
Results may differ from a plain program's by a relative error of at most 0.00024.
Values sent between devices are 32-bit elements; how exact they have to be, the bound alone decides.
A program may use at most 448 MiB of HBM per device.

v0:
```python
import jax
import jax.numpy as jnp
import numpy as np
from jax import lax
from jax.sharding import PartitionSpec as P


def passed_along(shard, axis, by):
    peers = lax.axis_size(axis)
    return lax.ppermute(shard, axis, [(i, (i + by) % peers) for i in range(peers)])


def offset_list():
    return [
        (step_x, step_y, step_z)
        for step_x in (-1, 0, 1)
        for step_y in (-1, 0, 1)
        for step_z in (-1, 0, 1)
        if (step_x, step_y, step_z) > (0, 0, 0)
    ]


def slot_number(offset):
    return offset_list().index(offset) + 1


def needed(side_x, side_y):
    chosen = [0]
    for position, offset in enumerate(offset_list()):
        if abs(side_x + offset[0]) <= 1 and abs(side_y + offset[1]) <= 1:
            chosen.append(position + 1)
    return chosen


def select_slots(blocks_in, slot_list, wanted):
    return jnp.concatenate(
        [
            blocks_in[:, slot_list.index(slot_id) : slot_list.index(slot_id) + 1]
            for slot_id in wanted
        ],
        axis=1,
    )


def first_slots(toward):
    merged = set()
    for across in (-1, 0, 1):
        merged.update(needed(toward, across))
    return sorted(merged)


def second_payload(held_data, toward):
    pieces = []
    layout = []
    for across in (-1, 0, 1):
        source = (across, 0)
        target = (across, toward)
        wanted = needed(target[0], target[1])
        blocks_in, slot_list = held_data[source]
        pieces.append(select_slots(blocks_in, slot_list, wanted))
        layout.append((target, wanted))
    return (jnp.concatenate(pieces, axis=1), layout)


def unpack(received, layout, lookup):
    cursor = 0
    for target, wanted in layout:
        lookup[target] = (received[:, cursor : cursor + len(wanted)], wanted)
        cursor += len(wanted)


def build_local(stored_blocks, onsite, bond_mask):
    blocks_here = stored_blocks[0, 0]
    layers = blocks_here.shape[0]
    block_size = blocks_here.shape[-1]
    leading = blocks_here[:, 0]
    identity = jnp.eye(block_size, dtype=jnp.float32)
    diagonal = (
        0.5 * (leading + jnp.swapaxes(leading, 1, 2)) + identity[None] * onsite[0, 0][:, None, :]
    )
    inside = np.array(
        [
            [1.0 if 0 <= layer_id + offset[2] < layers else 0.0 for offset in offset_list()]
            for layer_id in range(layers)
        ],
        np.float32,
    )
    keep_mask = bond_mask[0, 0].astype(jnp.float32) * inside
    others = blocks_here[:, 1:] * keep_mask[:, :, None, None]
    return (jnp.concatenate([diagonal[:, None], others], axis=1), keep_mask)


def fetch_block(lookup, cell_at, slot_id):
    blocks_in, slot_list = lookup[cell_at[0], cell_at[1]]
    return blocks_in[cell_at[2], slot_list.index(slot_id)]


def block_at(lookup, cell_at, offset, layers):
    if not 0 <= cell_at[2] < layers:
        return None
    if offset == (0, 0, 0):
        return (fetch_block(lookup, cell_at, 0), False)
    if offset > (0, 0, 0):
        if not 0 <= cell_at[2] + offset[2] < layers:
            return None
        return (fetch_block(lookup, cell_at, slot_number(offset)), False)
    source = (cell_at[0] + offset[0], cell_at[1] + offset[1], cell_at[2] + offset[2])
    if not 0 <= source[2] < layers:
        return None
    return (fetch_block(lookup, source, slot_number((-offset[0], -offset[1], -offset[2]))), True)


def oriented(term):
    block, flipped = term
    return jnp.swapaxes(block, 0, 1) if flipped else block


def square_all(lookup, layers, block_size):
    zero_block = jnp.zeros((block_size, block_size), jnp.float32)
    all_offsets = [
        (step_x, step_y, step_z)
        for step_x in (-1, 0, 1)
        for step_y in (-1, 0, 1)
        for step_z in (-1, 0, 1)
    ]
    results = []
    for target_offset in [(0, 0, 0)] + offset_list():
        middles = []
        for middle in all_offsets:
            remainder = (
                target_offset[0] - middle[0],
                target_offset[1] - middle[1],
                target_offset[2] - middle[2],
            )
            if max(abs(remainder[0]), abs(remainder[1]), abs(remainder[2])) <= 1:
                middles.append((middle, remainder))
        left_levels = []
        right_levels = []
        for layer_id in range(layers):
            left_parts = []
            right_parts = []
            for middle, remainder in middles:
                left_term = block_at(lookup, (0, 0, layer_id), middle, layers)
                right_term = block_at(
                    lookup, (middle[0], middle[1], layer_id + middle[2]), remainder, layers
                )
                if left_term is None or right_term is None:
                    left_parts.append(zero_block)
                    right_parts.append(zero_block)
                else:
                    left_parts.append(oriented(left_term))
                    right_parts.append(oriented(right_term))
            left_levels.append(jnp.concatenate(left_parts, axis=1))
            right_levels.append(jnp.concatenate(right_parts, axis=0))
        left_stack = jnp.stack(left_levels, axis=0)
        right_stack = jnp.stack(right_levels, axis=0)
        results.append(
            jnp.einsum(
                "lak,lkc->lac",
                left_stack,
                right_stack,
                precision=lax.Precision.HIGHEST,
                preferred_element_type=jnp.float32,
            )
        )
    return jnp.stack(results, axis=1)


def shards(stored_blocks, onsite, bond_mask):
    layers = stored_blocks.shape[2]
    block_size = stored_blocks.shape[-1]
    local_blocks, keep_mask = build_local(stored_blocks, onsite, bond_mask)
    own_slots = list(range(local_blocks.shape[1]))
    lookup = {(0, 0): (local_blocks, own_slots)}
    plus_slots = first_slots(1)
    minus_slots = first_slots(-1)
    lookup[1, 0] = (
        passed_along(select_slots(local_blocks, own_slots, plus_slots), "row", -1),
        plus_slots,
    )
    lookup[-1, 0] = (
        passed_along(select_slots(local_blocks, own_slots, minus_slots), "row", 1),
        minus_slots,
    )
    held_data = dict(lookup)
    payload, layout = second_payload(held_data, 1)
    unpack(passed_along(payload, "col", -1), layout, lookup)
    payload, layout = second_payload(held_data, -1)
    unpack(passed_along(payload, "col", 1), layout, lookup)
    diag_now = local_blocks[:, 0]
    trace_one = jnp.sum(jnp.trace(diag_now, axis1=1, axis2=2))
    squared = square_all(lookup, layers, block_size)
    diag_trace = jnp.sum(jnp.trace(squared[:, 0], axis1=1, axis2=2))
    trace_one, trace_two = lax.psum((trace_one, diag_trace), ("row", "col"))
    cell_count = lax.axis_size("row") * lax.axis_size("col") * layers
    target_fill = float(cell_count * block_size // 2)
    steering = jax.nn.sigmoid(
        (jnp.abs(trace_two - target_fill) - jnp.abs(2.0 * trace_one - trace_two - target_fill))
        / block_size
    )
    full_keep = jnp.concatenate([jnp.ones((layers, 1), jnp.float32), keep_mask], axis=1)
    result = full_keep[:, :, None, None] * (squared + 2.0 * steering * (local_blocks - squared))
    return result[None, None]


def solution(mesh):
    in_specs = (
        P("row", "col", None, None, None, None),
        P("row", "col", None, None),
        P("row", "col", None, None),
    )
    out_specs = P("row", "col", None, None, None, None)
    return jax.shard_map(shards, mesh=mesh, in_specs=in_specs, out_specs=out_specs, check_vma=False)
```

profile of v0, /device:TPU:0, one launch (start us, length us, event | category | flops | bytes accessed | tf_op | source)
XLA Modules:
  0.0 912.0 jit_solution(14082379041472025280)
XLA Ops:
  0.0 8.4 copy.5
  8.4 6.4 slice.329
  15.9 7.6 copy.7
  23.8 3.9 broadcast_multiply_fusion
  30.2 83.5 %collective-permute-done = f32[2,14,256,256]{3,2,1,0:T(8,128)S(1)} collective-permute-done((f32[2,14,256,256]{3,2,1,0:T(8,128)S(1)}, f32[2,14,256,256]{3,2,1,0:T(8,128)S(1)}, u32[]{:S(2)}, u32[]{:S(2)}) %collective-permute-start) | collective-permute-done | bytes 7340064 | tf_op jit(solution)/shard_map/ppermute | solution.py:10
  124.8 3.4 slice_dynamic-update-slice_fusion
  128.2 24.9 %collective-permute-done.1 = f32[2,5,256,256]{3,2,1,0:T(8,128)S(1)} collective-permute-done((f32[2,5,256,256]{3,2,1,0:T(8,128)S(1)}, f32[2,5,256,256]{3,2,1,0:T(8,128)S(1)}, u32[]{:S(2)}, u32[]{:S(2)}) %collective-permute-start.1) | collective-permute-done | bytes 2621472 | tf_op jit(solution)/shard_map/ppermute | solution.py:10
  154.9 15.2 %copy.8 = f32[2,27,256,256]{2,3,1,0:T(8,128)} copy(f32[2,27,256,256]{3,2,1,0:T(8,128)} %constant_dynamic-update-slice_fusion) | data formatting | bytes 28311552 | tf_op jit(solution)/shard_map/concatenate | solution.py:62
  172.6 4.4 collective-permute-start.3
  177.0 4.1 slice_bitcast_fusion.37
  233.6 6.6 fusion.213
  269.0 111.0 %collective-permute-done.3 = f32[2,18,256,256]{3,2,1,0:T(8,128)} collective-permute-done((f32[2,18,256,256]{3,2,1,0:T(8,128)}, f32[2,18,256,256]{3,2,1,0:T(8,128)}, u32[]{:S(2)}, u32[]{:S(2)}) %collective-permute-start.3) | collective-permute-done | bytes 9437216 | tf_op jit(solution)/shard_map/ppermute | solution.py:10
  380.0 3.9 slice_bitcast_fusion.2
  429.4 50.8 %collective-permute-done.2 = f32[2,27,256,256]{2,3,1,0:T(8,128)} collective-permute-done((f32[2,27,256,256]{2,3,1,0:T(8,128)}, f32[2,27,256,256]{2,3,1,0:T(8,128)}, u32[]{:S(2)}, u32[]{:S(2)}) %collective-permute-start.2) | collective-permute-done | bytes 14155808 | tf_op jit(solution)/shard_map/ppermute | solution.py:10
  480.3 4.0 slice_bitcast_fusion.10
  577.4 3.5 constant_dynamic-update-slice_fusion.547
  658.6 15.9 %constant_dynamic-update-slice_fusion.551 = (f32[1,1,2,14,256,256]{5,4,3,2,1,0:T(8,128)}, f32[2,256,256]{2,1,0:T(8,128)S(1)}) fusion(f32[1,6912,256]{2,1,0:T(8,128)} %bitcast.78, f32[1,6912,256]{2,1,0:T(8,128)S(1)} %bitcast.993, f32[1,256,6912]{2,1,0:T(8,128)S(1)} %bitcast.994, f32[1,256,6912]{2,1,0:T(8,128)S(1)} %bitcast.990), kind=kOutput, calls=%fused_computation.651 | convolution fusion | flops 10878713856 | bytes 29360128 | tf_op jit(solution)/shard_map/lak,lkc->lac/dot_general | solution.py:158
  675.4 64.3 %all-reduce.19 = (f32[]{:T(128)}, f32[]{:T(128)}) all-reduce(f32[]{:T(128)} %get-tuple-element.6, f32[]{:T(128)} %get-tuple-element.5), channel_id=1, replica_groups=mesh['row'=8,'col'=16] {'row','col'}, use_global_device_ids=true, to_apply=%region_1.2 | all-reduce | flops 2 | bytes 16 | tf_op jit(solution)/shard_map/psum | solution.py:194
  800.8 13.4 %fusion.70 = f32[1,1,2,14,256,256]{5,4,3,2,1,0:T(8,128)S(1)} fusion(f32[1,1,2,14,256,256]{5,4,3,2,1,0:T(8,128)S(1)} %bitcast.976, f32[1,4608,256]{1,2,0:T(8,128)S(1)} %bitcast.977, f32[256,4608]{1,0:T(8,128)} %get-tuple-element.186), kind=kOutput, calls=%fused_computation.75 | convolution fusion | flops 3623878656 | bytes 9961472 | tf_op jit(solution)/shard_map/lak,lkc->lac/dot_general | solution.py:158
  814.2 8.0 fusion.160
  822.2 16.7 %fusion.150 = f32[1,1,2,14,256,256]{5,4,3,2,1,0:T(8,128)S(1)} fusion(f32[1,1,2,14,256,256]{5,4,3,2,1,0:T(8,128)S(1)} %fusion.160, f32[1,4608,256]{2,1,0:T(8,128)} %bitcast.142, f32[1,4608,256]{2,1,0:T(8,128)} %bitcast.128, f32[1,256,4608]{2,1,0:T(8,128)} %bitcast.122, f32[1,256,4608]{2,1,0:T(8,128)} %bitcast.121), kind=kOutput, calls=%fused_computation.91 | convolution fusion | flops 7252475904 | bytes 19398656 | tf_op jit(solution)/shard_map/lak,lkc->lac/dot_general | solution.py:158
  838.9 7.2 fusion.170
  846.1 4.5 fusion.80
  850.7 8.2 fusion.130
  858.9 4.6 fusion.90
  863.6 4.0 fusion.180
  867.7 11.6 %fusion.140 = f32[1,1,2,14,256,256]{5,4,3,2,1,0:T(8,128)S(1)} fusion(f32[1,1,2,14,256,256]{5,4,3,2,1,0:T(8,128)S(1)} %fusion.180, f32[1,4608,256]{1,2,0:T(8,128)S(1)} %bitcast.981, f32[1,4608,256]{1,2,0:T(8,128)S(1)} %bitcast.978, f32[1,256,4608]{2,1,0:T(8,128)S(1)} %bitcast.984, f32[1,256,4608]{2,1,0:T(8,128)} %bitcast.197), kind=kOutput, calls=%fused_computation.89 | convolution fusion | flops 7252475904 | bytes 19398656 | tf_op jit(solution)/shard_map/lak,lkc->lac/dot_general | solution.py:158
  879.3 7.1 fusion.190
  886.4 4.9 fusion.100
  891.3 11.8 %fusion.120 = f32[1,1,2,14,256,256]{5,4,3,2,1,0:T(8,128)S(1)} fusion(f32[1,1,2,14,256,256]{5,4,3,2,1,0:T(8,128)S(1)} %fusion.100, f32[1,3072,256]{2,1,0:T(8,128)} %bitcast.227, f32[1,3072,256]{2,1,0:T(8,128)} %bitcast.225, f32[1,256,3072]{2,1,0:T(8,128)} %bitcast.224, f32[1,256,3072]{2,1,0:T(8,128)} %bitcast.223), kind=kOutput, calls=%fused_computation.85 | convolution fusion | flops 4834983936 | bytes 13107200 | tf_op jit(solution)/shard_map/lak,lkc->lac/dot_general | solution.py:158
  903.1 5.1 fusion.110
  908.2 3.7 fusion.25
  (553 shorter events, 375.7 us)
Async XLA Ops:
  27.8 97.0 %copy-start = (f32[2,13,256,256]{3,2,1,0:T(8,128)}, f32[2,13,256,256]{3,2,1,0:T(8,128)S(1)}, u32[]{:S(2)}) copy-start(f32[2,13,256,256]{3,2,1,0:T(8,128)S(1)} %broadcast_multiply_fusion) | copy-start | bytes 20447236
  30.1 83.5 %collective-permute-start = (f32[2,14,256,256]{3,2,1,0:T(8,128)S(1)}, f32[2,14,256,256]{3,2,1,0:T(8,128)S(1)}, u32[]{:S(2)}, u32[]{:S(2)}) collective-permute-start(f32[2,14,256,256]{3,2,1,0:T(8,128)S(1)} %pad_maximum_fusion), channel_id=1, source_target_pairs={{0,16},{16,32},{32,48},{48,64},{64,80},{80,96},{96,112},{112,0},{1... | collective-permute-start | bytes 22020104 | tf_op jit(solution)/shard_map/ppermute | solution.py:10
  123.9 29.2 %collective-permute-start.1 = (f32[2,5,256,256]{3,2,1,0:T(8,128)S(1)}, f32[2,5,256,256]{3,2,1,0:T(8,128)S(1)}, u32[]{:S(2)}, u32[]{:S(2)}) collective-permute-start(f32[2,5,256,256]{3,2,1,0:T(8,128)S(1)} %pad_maximum_fusion.1), channel_id=1, source_target_pairs={{0,112},{16,0},{32,16},{48,32},{64,48},{80,64},{96,80},{112,96},{1... | collective-permute-start | bytes 7864328 | tf_op jit(solution)/shard_map/ppermute | solution.py:10
  170.1 310.2 %collective-permute-start.2 = (f32[2,27,256,256]{2,3,1,0:T(8,128)}, f32[2,27,256,256]{2,3,1,0:T(8,128)}, u32[]{:S(2)}, u32[]{:S(2)}) collective-permute-start(f32[2,27,256,256]{2,3,1,0:T(8,128)} %copy.8), channel_id=1, source_target_pairs={{0,1},{1,2},{2,3},{3,4},{4,5},{5,6},{6,7},{7,8},{8,9},{9,10},{10,1... | collective-permute-start | bytes 42467336 | tf_op jit(solution)/shard_map/ppermute | solution.py:10
  172.6 207.3 %collective-permute-start.3 = (f32[2,18,256,256]{3,2,1,0:T(8,128)}, f32[2,18,256,256]{3,2,1,0:T(8,128)}, u32[]{:S(2)}, u32[]{:S(2)}) collective-permute-start(f32[2,18,256,256]{3,2,1,0:T(8,128)} %constant_dynamic-update-slice_fusion.3), channel_id=1, source_target_pairs={{0,15},{1,0},{2,1},{3,2},{4,3},{5,4},{6,5},{7,6},{8,7},{9,8},{10,9... | collective-permute-start | bytes 28311560 | tf_op jit(solution)/shard_map/ppermute | solution.py:10
  244.4 24.6 %copy-start.28 = (f32[256,256]{1,0:T(8,128)}, f32[256,256]{1,0:T(8,128)S(1)}, u32[]{:S(2)}) copy-start(f32[256,256]{1,0:T(8,128)S(1)} %copy.16) | copy-start | bytes 786436
  575.0 13.3 %copy-start.1 = (f32[256,3072]{1,0:T(8,128)}, f32[256,3072]{1,0:T(8,128)S(1)}, u32[]{:S(2)}) copy-start(f32[256,3072]{1,0:T(8,128)S(1)} %get-tuple-element.180) | copy-start | bytes 9437188
  575.0 14.2 %copy-start.10 = (f32[256,4608]{1,0:T(8,128)}, f32[256,4608]{1,0:T(8,128)S(1)}, u32[]{:S(2)}) copy-start(f32[256,4608]{1,0:T(8,128)S(1)} %get-tuple-element.181) | copy-start | bytes 14155780
  575.0 14.2 %copy-start.72 = (f32[256,6912]{1,0:T(8,128)}, f32[256,6912]{1,0:T(8,128)S(1)}, u32[]{:S(2)}) copy-start(f32[256,6912]{1,0:T(8,128)S(1)} %get-tuple-element.178) | copy-start | bytes 21233668
  617.1 36.3 %copy-start.73 = (f32[256,6912]{1,0:T(8,128)S(1)}, f32[256,6912]{1,0:T(8,128)}, u32[]{:S(2)}) copy-start(f32[256,6912]{1,0:T(8,128)} %copy-done.72) | copy-start | bytes 21233668
  618.6 24.2 %slice-start.10 = ((s8[7077888]{0:T(1024)(128)(4,1)}), s8[4194304]{0:T(1024)(128)(4,1)S(1)}, s32[]{:S(2)}) async-start(s8[7077888]{0:T(1024)(128)(4,1)} %bitcast.991), calls=%async_computation.10 | async-start | bytes 8388608
  626.1 16.7 %copy-start.21 = (f32[256,256]{1,0:T(8,128)S(1)}, f32[256,256]{1,0:T(8,128)}, u32[]{:S(2)}) copy-start(f32[256,256]{1,0:T(8,128)} %copy.26) | copy-start | bytes 786436
  628.6 14.3 %copy-start.69 = (f32[256,256]{0,1:T(8,128)S(1)}, f32[256,256]{0,1:T(8,128)}, u32[]{:S(2)}) copy-start(f32[256,256]{0,1:T(8,128)} %copy.28) | copy-start | bytes 786436
  628.6 14.3 %slice-start.11 = ((s8[7077888]{0:T(1024)(128)(4,1)}), s8[2883584]{0:T(1024)(128)(4,1)S(1)}, s32[]{:S(2)}) async-start(s8[7077888]{0:T(1024)(128)(4,1)} %bitcast.991), calls=%async_computation.11 | async-start | bytes 5767168
  628.6 14.4 %copy-start.68 = (f32[256,256]{0,1:T(8,128)S(1)}, f32[256,256]{0,1:T(8,128)}, u32[]{:S(2)}) copy-start(f32[256,256]{0,1:T(8,128)} %copy.29) | copy-start | bytes 786436
  631.0 12.0 %copy-start.67 = (f32[256,256]{0,1:T(8,128)S(1)}, f32[256,256]{0,1:T(8,128)}, u32[]{:S(2)}) copy-start(f32[256,256]{0,1:T(8,128)} %copy.30) | copy-start | bytes 786436
  631.0 12.1 %copy-start.66 = (f32[256,256]{0,1:T(8,128)S(1)}, f32[256,256]{0,1:T(8,128)}, u32[]{:S(2)}) copy-start(f32[256,256]{0,1:T(8,128)} %copy.31) | copy-start | bytes 786436
  741.4 12.0 %copy-start.19 = (f32[256,256]{0,1:T(8,128)S(1)}, f32[256,256]{0,1:T(8,128)}, u32[]{:S(2)}) copy-start(f32[256,256]{0,1:T(8,128)} %copy.33) | copy-start | bytes 786436
  741.5 12.0 %copy-start.16 = (f32[256,256]{0,1:T(8,128)S(1)}, f32[256,256]{0,1:T(8,128)}, u32[]{:S(2)}) copy-start(f32[256,256]{0,1:T(8,128)} %copy.67) | copy-start | bytes 786436
  741.5 12.1 %copy-start.14 = (f32[1,1,256,256]{2,3,1,0:T(8,128)S(1)}, f32[1,1,256,256]{2,3,1,0:T(8,128)}, u32[]{:S(2)}) copy-start(f32[1,1,256,256]{2,3,1,0:T(8,128)} %copy.184) | copy-start | bytes 786436
  762.7 12.1 %copy-start.43 = (f32[1,1,256,256]{2,3,1,0:T(8,128)S(1)}, f32[1,1,256,256]{2,3,1,0:T(8,128)}, u32[]{:S(2)}) copy-start(f32[1,1,256,256]{2,3,1,0:T(8,128)} %copy.178) | copy-start | bytes 786436
  778.8 22.0 %slice-start.4 = ((s8[7340032]{0:T(1024)(128)(4,1)}), s8[4194304]{0:T(1024)(128)(4,1)S(1)}, s32[]{:S(2)}) async-start(s8[7340032]{0:T(1024)(128)(4,1)} %bitcast.975), calls=%async_computation.4 | async-start | bytes 8388608
  779.9 16.8 %copy-start.49 = (f32[256,256]{0,1:T(8,128)S(1)}, f32[256,256]{0,1:T(8,128)}, u32[]{:S(2)}) copy-start(f32[256,256]{0,1:T(8,128)} %copy.68) | copy-start | bytes 786436
  781.1 16.4 %copy-start.50 = (f32[256,256]{0,1:T(8,128)S(1)}, f32[256,256]{0,1:T(8,128)}, u32[]{:S(2)}) copy-start(f32[256,256]{0,1:T(8,128)} %copy.69) | copy-start | bytes 786436
  782.2 16.1 %copy-start.40 = (f32[256,256]{0,1:T(8,128)S(1)}, f32[256,256]{0,1:T(8,128)}, u32[]{:S(2)}) copy-start(f32[256,256]{0,1:T(8,128)} %copy.157) | copy-start | bytes 786436
  784.2 14.9 %copy-start.42 = (f32[1,1,256,256]{2,3,1,0:T(8,128)S(1)}, f32[1,1,256,256]{2,3,1,0:T(8,128)}, u32[]{:S(2)}) copy-start(f32[1,1,256,256]{2,3,1,0:T(8,128)} %copy.181) | copy-start | bytes 786436
  785.2 14.7 %copy-start.41 = (f32[1,1,256,256]{2,3,1,0:T(8,128)S(1)}, f32[1,1,256,256]{2,3,1,0:T(8,128)}, u32[]{:S(2)}) copy-start(f32[1,1,256,256]{2,3,1,0:T(8,128)} %copy.182) | copy-start | bytes 786436
  788.5 12.3 %slice-start.5 = ((s8[7340032]{0:T(1024)(128)(4,1)}), s8[3145728]{0:T(1024)(128)(4,1)S(1)}, s32[]{:S(2)}) async-start(s8[7340032]{0:T(1024)(128)(4,1)} %bitcast.975), calls=%async_computation.5 | async-start | bytes 6291456
  788.5 12.3 %copy-start.22 = (f32[3072,256]{0,1:T(8,128)}, f32[3072,256]{0,1:T(8,128)S(1)}, u32[]{:S(2)}) copy-start(f32[3072,256]{0,1:T(8,128)S(1)} %get-tuple-element.324) | copy-start | bytes 9437188
  788.6 12.2 %copy-start.9 = (f32[4608,256]{0,1:T(8,128)}, f32[4608,256]{0,1:T(8,128)S(1)}, u32[]{:S(2)}) copy-start(f32[4608,256]{0,1:T(8,128)S(1)} %constant_dynamic-update-slice_fusion.429) | copy-start | bytes 14155780
  891.2 16.9 %slice-start.2 = ((s8[6815744]{0:T(1024)(128)(4,1)}), s8[4194304]{0:T(1024)(128)(4,1)S(1)}, s32[]{:S(2)}) async-start(s8[6815744]{0:T(1024)(128)(4,1)} %bitcast.972), calls=%async_computation.2 | async-start | bytes 8388608
  891.3 16.9 %slice-start.3 = ((s8[6815744]{0:T(1024)(128)(4,1)}), s8[2621440]{0:T(1024)(128)(4,1)S(1)}, s32[]{:S(2)}) async-start(s8[6815744]{0:T(1024)(128)(4,1)} %bitcast.972), calls=%async_computation.3 | async-start | bytes 5242880
  (61 other events, 395.6 us)
where the time goes:
time: 922 us; the launch traced here: 912 us
  local copies, waits for them, and re-layouts  427 us (46%)
  waiting for transfers between devices  270 us (29%)
  matrix products  123 us (13%)
  blocking collectives  64.3 us (7%)
  other arithmetic  17.7 us (2%)
    ppermute x4, waiting for transfers between devices, passed_along(): lax.ppermute(shard, axis, [(i, (i + by) % peers) for i in range(peers)])  270 us
    unnamed x459, local copies, waits for them, and re-layouts  267 us
    dot_general x14, matrix products, square_all(): jnp.einsum('lak,lkc->lac', left_stack, right_stack, precision=lax.Precisi...  123 us
    squeeze x41, local copies, waits for them, and re-layouts, fetch_block(): return blocks_in[cell_at[2], slot_list.index(slot_id)]  77.1 us
    psum x1, blocking collectives, shards(): trace_one, trace_two = lax.psum((trace_one, diag_trace), ('row', 'col'))  64.3 us
    transpose x16, local copies, waits for them, and re-layouts, oriented(): return jnp.swapaxes(block, 0, 1) if flipped else block  27.1 us
  transfers between devices with their start and end apart: 4, of which 4 were waited for; matrix products, arithmetic and copies ran while one was open for 16% of the time, Pallas kernels for 0%

commit v1 on v0

v1 whole, which is shorter than its diff:
```python
import jax
import jax.numpy as jnp
from jax import lax
from jax.experimental import pallas as pl
from jax.experimental.pallas import tpu as pltpu
from jax.sharding import PartitionSpec as P

MESH = pl.DeviceIdType.MESH
F32 = jnp.float32
BF16 = jnp.bfloat16
B = 256
W2 = 2 * B

DG, ER, ML, ZD, PR = range(5)
MIDDLE = {ER: 3, ML: 6, ZD: 9, PR: 12}
QQ = 5

(P_L, E_L, Q_L, M_R, Z_R, D_R, Z_U, P_U, P_UL, M_UR, Z_UR, E_W, D_W, E_WL, D_WR) = range(15)
NRX = 15
ET = 5


def sp(rx):
    return 6 + rx


QUADS = ((0, 0), (0, 1), (1, 0), (1, 1))
DQUADS = (0, 1, 3)


def block_slot(t, z, z2):
    return MIDDLE[t] + z2 - z


def kernel(stored, onsite, mask, out, own, rx, hi, lo, y, zero, part, gath, steer,
           in_sem, out_sem, send_sem, recv_sem, ar_send, ar_recv):
    row = lax.axis_index("row")
    col = lax.axis_index("col")
    nrow = lax.axis_size("row")
    ncol = lax.axis_size("col")
    right = (row, lax.rem(col + 1, ncol))
    left = (row, lax.rem(col + ncol - 1, ncol))
    down = (lax.rem(row + 1, nrow), col)
    up = (lax.rem(row + nrow - 1, nrow), col)
    xs = lax.rem(col, 4)
    ys = col // 4
    cs = lax.rem(row, 2)
    zs = row // 2
    x_peers = [(row, ys * 4 + lax.rem(xs + j, 4)) for j in (1, 2, 3)]
    y_peers = [(row, lax.rem(ys + j, 4) * 4 + xs) for j in (1, 2, 3)]
    z_peers = [(lax.rem(zs + j, 4) * 2 + cs, col) for j in (1, 2, 3)]
    core_peer = (zs * 2 + 1 - cs, col)

    loads = {}
    for t in (PR, ML, ER, ZD):
        for q, (z, z2) in enumerate(QUADS):
            loads[t, q] = pltpu.make_async_copy(
                stored.at[z, block_slot(t, z, z2)],
                own.at[t, pl.ds(z * B, B), pl.ds(z2 * B, B)],
                in_sem.at[(t - 1) * 4 + q],
            )
    for n, (q, z, slot) in enumerate(((0, 0, 0), (1, 0, 1), (3, 1, 0))):
        i, j = QUADS[q]
        loads[DG, q] = pltpu.make_async_copy(
            stored.at[z, slot], own.at[DG, pl.ds(i * B, B), pl.ds(j * B, B)], in_sem.at[16 + n]
        )
    for copy in loads.values():
        copy.start()

    barrier = pltpu.get_barrier_semaphore()
    greeted = [right, left, down, up] + x_peers + y_peers + z_peers + [core_peer]
    for peer in greeted:
        pl.semaphore_signal(barrier, inc=1, device_id=peer, device_id_type=MESH)

    zero[...] = jnp.zeros_like(zero)

    def put_split(k, rows, cols, value):
        high = value.astype(BF16)
        hi[k, rows, cols] = high
        lo[k, rows, cols] = (value - high.astype(F32)).astype(BF16)

    def strips(start, strip):
        return pl.ds(pl.multiple_of(start + strip, 8), 64)

    squares = jnp.zeros((8, B), F32)
    for t in (PR, ML, ER, ZD):
        for q, (z, z2) in enumerate(QUADS):
            loads[t, q].wait()
            keep = mask[z, block_slot(t, z, z2) - 1].astype(F32)
            cols = pl.ds(z2 * B, B)

            def strip_step(s, total, t=t, z=z, cols=cols, keep=keep):
                rows = pl.ds(pl.multiple_of(z * B + s * 64, 64), 64)
                value = own[t, rows, cols] * keep
                own[t, rows, cols] = value
                put_split(t, rows, cols, value)
                return total + jnp.sum((value * value).reshape(8, 8, B), axis=0)

            squares = lax.fori_loop(0, 4, strip_step, squares)
    squares = 2.0 * squares
    trace = jnp.zeros((8, B), F32)
    diag = lax.broadcasted_iota(jnp.int32, (B, B), 0) == lax.broadcasted_iota(jnp.int32, (B, B), 1)
    for z, q in ((0, 0), (1, 3)):
        loads[DG, q].wait()
        here = pl.ds(z * B, B)
        raw = own[DG, here, here]
        value = 0.5 * (raw + raw.T) + jnp.where(diag, onsite[z : z + 1, :], 0.0)
        own[DG, here, here] = value
        put_split(DG, here, here, value)
        squares = squares + jnp.sum((value * value).reshape(32, 8, B), axis=0)
        trace = trace + jnp.sum(jnp.where(diag, value, 0.0).reshape(32, 8, B), axis=0)
    loads[DG, 1].wait()
    top, low = pl.ds(0, B), pl.ds(B, B)
    value = own[DG, top, low] * mask[0, 0].astype(F32)
    own[DG, top, low] = value
    put_split(DG, top, low, value)
    squares = squares + 2.0 * jnp.sum((value * value).reshape(32, 8, B), axis=0)
    flipped = value.T
    own[DG, low, top] = flipped
    put_split(DG, low, top, flipped)
    part[0, 0:8, :] = trace
    part[0, 8:16, :] = squares

    pl.semaphore_wait(barrier, len(greeted))

    small = []

    def send_part(stage, peers, base):
        copies = []
        for n, peer in enumerate(peers):
            copy = pltpu.make_async_remote_copy(
                src_ref=part.at[stage],
                dst_ref=gath.at[base + n],
                send_sem=ar_send.at[base + n],
                recv_sem=ar_recv.at[base + n],
                device_id=peer,
                device_id_type=MESH,
            )
            copy.start()
            copies.append(copy)
        small.extend(copies)
        return copies

    def add_parts(stage, copies, base):
        total = part[stage]
        for n, copy in enumerate(copies):
            copy.wait_recv()
            total = total + gath[base + n]
        part[stage + 1] = total

    sent = {}

    def send(source, rxi, q, peer):
        i, j = QUADS[q]
        where = (pl.ds(i * B, B), pl.ds(j * B, B))
        copy = pltpu.make_async_remote_copy(
            src_ref=source(*where),
            dst_ref=rx.at[(rxi,) + where],
            send_sem=send_sem.at[rxi * 4 + q],
            recv_sem=recv_sem.at[rxi * 4 + q],
            device_id=peer,
            device_id_type=MESH,
        )
        copy.start()
        sent[rxi, q] = copy

    def from_own(t):
        return lambda rows, cols: own.at[t, rows, cols]

    def from_rx(k):
        return lambda rows, cols: rx.at[k, rows, cols]

    def from_y(k):
        return lambda rows, cols: y.at[k, rows, cols]

    def prep(rxi, q, flip=False, keep=True):
        i, j = QUADS[q]

        def strip_step(s, carry):
            offset = pl.multiple_of(s * 128, 128)
            value = rx[rxi, pl.ds(i * B + offset, 128), pl.ds(j * B, B)]
            if keep:
                put_split(sp(rxi), pl.ds(i * B + offset, 128), pl.ds(j * B, B), value)
            if flip:
                put_split(sp(rxi), pl.ds(j * B, B), pl.ds(i * B + offset, 128), value.T)
            return carry

        lax.fori_loop(0, 2, strip_step, 0)

    def take(rxi, quads=range(4), forward=None, **how):
        for q in quads:
            sent[rxi, q].wait_recv()
            if forward is not None:
                send(from_rx(rxi), forward[0], q, forward[1])
            prep(rxi, q, **how)

    def take_t(rxi, quads=range(4), forward=None):
        take(rxi, quads, forward, flip=True, keep=False)

    def take_d(rxi, quads=DQUADS, forward=None):
        for q in quads:
            take(rxi, (q,), forward, flip=q == 1)

    def products(yi, terms, first=False):
        def tile(step, carry):
            if yi == DG:
                m, n = step // 2, (step + 1) // 2
            else:
                m, n = step // 2, step % 2
            rows = pl.ds(pl.multiple_of(m * B, B), B)
            cols = pl.ds(pl.multiple_of(n * B, B), B)
            total = None if first else y[yi, rows, cols]
            for a, b, turned in terms:
                a_hi = hi[a, rows, :]
                a_lo = lo[a, rows, :]
                if turned:
                    b_hi, b_lo = hi[b, cols, :], lo[b, cols, :]
                    dims = (((1,), (1,)), ((), ()))
                else:
                    b_hi, b_lo = hi[b, :, cols], lo[b, :, cols]
                    dims = (((1,), (0,)), ((), ()))
                for u, v in ((a_hi, b_hi), (a_hi, b_lo), (a_lo, b_hi)):
                    term = lax.dot_general(u, v, dims, preferred_element_type=F32)
                    total = term if total is None else total + term
            y[yi, rows, cols] = total
            return carry

        lax.fori_loop(0, 3 if yi == DG else 4, tile, 0)

    outs = []

    def finish(yi, extra=None):
        quads = DQUADS if yi == DG else range(4)
        for q in quads:
            z, z2 = QUADS[q]
            if yi == DG:
                slot = 1 if q == 1 else 0
            else:
                slot = block_slot(yi, z, z2)
            if extra is not None:
                sent[extra, q].wait_recv()
            keep = mask[z, slot - 1].astype(F32) if slot else None

            def strip_step(s, carry, z=z, z2=z2, keep=keep):
                rows = pl.ds(pl.multiple_of(z * B + s * 64, 64), 64)
                cols = pl.ds(z2 * B, B)
                value = y[yi, rows, cols]
                if extra is not None:
                    value = value + rx[extra, rows, cols]
                value = value + steer[0:1, :] * (own[yi, rows, cols] - value)
                if keep is not None:
                    value = value * keep
                y[yi, rows, cols] = value
                return carry

            lax.fori_loop(0, 4, strip_step, 0)
            copy = pltpu.make_async_copy(
                y.at[yi, pl.ds(z * B, B), pl.ds(z2 * B, B)],
                out.at[z, slot],
                out_sem.at[z * 14 + slot],
            )
            copy.start()
            outs.append(copy)

    x_parts = send_part(0, x_peers, 0)
    for q in range(4):
        send(from_own(PR), P_L, q, right)
        send(from_own(ML), M_R, q, left)
    for q in range(4):
        send(from_own(ER), E_L, q, right)
        send(from_own(ZD), Z_R, q, left)
    for q in DQUADS:
        send(from_own(DG), D_R, q, left)

    for z, slots in ((0, (2, 5, 8, 11)), (1, (1, 4, 7, 10, 13))):
        for slot in slots:
            copy = pltpu.make_async_copy(zero, out.at[z, slot], out_sem.at[z * 14 + slot])
            copy.start()
            outs.append(copy)

    products(ER, [(DG, ER, False)], first=True)
    add_parts(0, x_parts, 0)
    z_parts = send_part(1, z_peers, 3)

    for q in range(4):
        send(from_own(ZD), Z_U, q, down)
        send(from_own(ER), E_W, q, up)
    for q in DQUADS:
        send(from_own(DG), D_W, q, up)
    for q in range(4):
        send(from_own(PR), P_U, q, down)

    for q, (i, j) in enumerate(QUADS):
        value = own[ER, pl.ds(i * B, B), pl.ds(j * B, B)].T
        put_split(ET, pl.ds(j * B, B), pl.ds(i * B, B), value)

    products(QQ, [(ET, ZD, False)], first=True)
    add_parts(1, z_parts, 3)
    y_parts = send_part(2, y_peers, 6)
    products(DG, [(DG, DG, False), (ER, ER, True), (ML, ML, True)], first=True)
    add_parts(2, y_parts, 6)
    core_part = send_part(3, [core_peer], 9)

    take(P_L, (0,), (P_UL, down))
    take(M_R, (0,), (M_UR, down))
    products(DG, [(ZD, ZD, True), (PR, PR, True)])
    core_part[0].wait_recv()
    total = part[3] + gath[9]
    t1 = jnp.sum(total[0:8, :])
    t2 = jnp.sum(total[8:16, :])
    goal = float(nrow * ncol * B)
    lean = (jnp.abs(t2 - goal) - jnp.abs(2.0 * t1 - t2 - goal)) / B
    steer[...] = 2.0 / (1.0 + jnp.exp(-jnp.full((8, B), lean, F32)))

    take(P_L, (1,), (P_UL, down))
    take(M_R, (1,), (M_UR, down))
    products(ML, [(DG, ML, False)], first=True)
    products(ZD, [(DG, ZD, False)], first=True)
    take(P_L, (2,), (P_UL, down))
    take(M_R, (2,), (M_UR, down))
    products(PR, [(DG, PR, False)], first=True)
    take_d(D_W)
    take(P_L, (3,), (P_UL, down))
    take(M_R, (3,), (M_UR, down))
    products(QQ, [(sp(M_R), sp(D_W), False)])
    for q in range(4):
        send(from_y(QQ), Q_L, q, right)

    take(E_W)
    take_t(Z_U)
    take(P_U)
    take_t(E_L, (0,), (E_WL, up))
    take(Z_R, (0,), (Z_UR, down))
    products(ZD, [(ZD, sp(D_W), False), (ER, sp(M_R), False), (PR, sp(E_W), True)])
    take_t(E_L, (1,), (E_WL, up))
    take(Z_R, (1,), (Z_UR, down))
    products(ER, [(ZD, sp(M_R), True), (sp(Z_U), sp(P_U), False)])
    products(PR, [(ZD, sp(E_W), False)])
    take_t(E_L, (2,), (E_WL, up))
    take(Z_R, (2,), (Z_UR, down))
    products(DG, [(sp(Z_U), sp(Z_U), True)])
    take_t(E_L, (3,), (E_WL, up))
    take(Z_R, (3,), (Z_UR, down))
    products(ZD, [(sp(E_L), sp(P_L), False)])
    products(ER, [(PR, sp(Z_R), True)])
    take_t(P_UL)
    take_t(M_UR)
    take_d(D_R, (0,), (D_WR, up))
    products(PR, [(ER, sp(Z_R), False)])
    take_d(D_R, (1,), (D_WR, up))
    products(DG, [(sp(E_L), sp(E_L), True), (sp(P_UL), sp(P_UL), True), (sp(M_UR), sp(M_UR), True)])
    take_d(D_R, (3,), (D_WR, up))
    finish(DG)
    take(Z_UR)
    products(ER, [(ER, sp(D_R), False), (sp(M_UR), sp(Z_UR), False)])
    finish(ER)
    take(E_WL)
    products(ZD, [(ML, sp(E_WL), False)])
    finish(ZD)
    products(ML, [(ZD, sp(E_WL), True)])
    take_d(D_WR)
    products(PR, [(PR, sp(D_WR), False)])
    finish(PR)
    finish(ML, Q_L)

    for copy in outs:
        copy.wait()
    for copy in small:
        copy.wait_send()
    for copy in sent.values():
        copy.wait_send()


def shards(stored_blocks, onsite, bond_mask):
    shape = stored_blocks.shape
    result = pl.pallas_call(
        kernel,
        out_shape=jax.ShapeDtypeStruct(shape[2:], F32),
        in_specs=[
            pl.BlockSpec(memory_space=pl.ANY),
            pl.BlockSpec(memory_space=pltpu.VMEM),
            pl.BlockSpec(memory_space=pltpu.SMEM),
        ],
        out_specs=pl.BlockSpec(memory_space=pl.ANY),
        scratch_shapes=[
            pltpu.VMEM((5, W2, W2), F32),
            pltpu.VMEM((NRX, W2, W2), F32),
            pltpu.VMEM((6 + NRX, W2, W2), BF16),
            pltpu.VMEM((6 + NRX, W2, W2), BF16),
            pltpu.VMEM((6, W2, W2), F32),
            pltpu.VMEM((B, B), F32),
            pltpu.VMEM((4, 16, B), F32),
            pltpu.VMEM((10, 16, B), F32),
            pltpu.VMEM((8, B), F32),
            pltpu.SemaphoreType.DMA((19,)),
            pltpu.SemaphoreType.DMA((28,)),
            pltpu.SemaphoreType.DMA((NRX * 4,)),
            pltpu.SemaphoreType.DMA((NRX * 4,)),
            pltpu.SemaphoreType.DMA((10,)),
            pltpu.SemaphoreType.DMA((10,)),
        ],
        compiler_params=pltpu.CompilerParams(
            collective_id=0, has_side_effects=True, vmem_limit_bytes=62 * 1024 * 1024
        ),
        name="sp2_step",
    )(stored_blocks[0, 0], onsite[0, 0], bond_mask[0, 0])
    return result[None, None]


def solution(mesh):
    in_specs = (
        P("row", "col", None, None, None, None),
        P("row", "col", None, None),
        P("row", "col", None, None),
    )
    out_specs = P("row", "col", None, None, None, None)
    return jax.shard_map(shards, mesh=mesh, in_specs=in_specs, out_specs=out_specs, check_vma=False)
```

time: 922 us -> 127 us (0.14)
  the two profiles are of different devices: /device:TPU:0 before, /device:TPU:30 now
where the time goes in v1:
time: 127 us; the launch traced here: 126 us
  Pallas kernels  119 us (94%)
  local copies, waits for them, and re-layouts  6.93 us (5%)
    pallas_call x1, Pallas kernels, shards(): pl.pallas_call(kernel, out_shape=jax.ShapeDtypeStruct(shape[2:], F32), in...  119 us
    unnamed x1, local copies, waits for them, and re-layouts  6.93 us

profile of v1, /device:TPU:30, one launch (start us, length us, event | category | flops | bytes accessed | tf_op | source)
XLA Modules:
  0.0 126.4 jit_solution(4022139110008931513)
XLA Ops:
  0.0 119.5 %sp2_step.1 = f32[2,14,256,256]{3,2,1,0:T(8,128)} custom-call(f32[2,14,256,256]{3,2,1,0:T(8,128)} %bitcast.5, f32[2,256]{1,0:T(2,128)} %bitcast.6, s32[2,13]{1,0:T(2,128)} %bitcast.7), custom_call_target="tpu_custom_call" | custom-call | tf_op jit(solution)/shard_map/sp2_step/pallas_call | solution.py:376
  119.5 6.9 %copy.5 = f32[1,1,2,14,256,256]{5,4,3,2,1,0:T(8,128)} copy(f32[1,1,2,14,256,256]{5,4,3,2,1,0:T(8,128)} %bitcast.4) | data formatting | bytes 14680064

commit v2 on v1

--- a/solution.py
+++ b/solution.py
@@ -42,14 +42,8 @@
     left = (row, lax.rem(col + ncol - 1, ncol))
     down = (lax.rem(row + 1, nrow), col)
     up = (lax.rem(row + nrow - 1, nrow), col)
-    xs = lax.rem(col, 4)
-    ys = col // 4
-    cs = lax.rem(row, 2)
-    zs = row // 2
-    x_peers = [(row, ys * 4 + lax.rem(xs + j, 4)) for j in (1, 2, 3)]
-    y_peers = [(row, lax.rem(ys + j, 4) * 4 + xs) for j in (1, 2, 3)]
-    z_peers = [(lax.rem(zs + j, 4) * 2 + cs, col) for j in (1, 2, 3)]
-    core_peer = (zs * 2 + 1 - cs, col)
+    col_peers = [(row, lax.rem(col + j, ncol)) for j in range(1, ncol)]
+    row_peers = [(lax.rem(row + j, nrow), col) for j in range(1, nrow)]
 
     loads = {}
     for t in (PR, ML, ER, ZD):
@@ -68,7 +62,7 @@
         copy.start()
 
     barrier = pltpu.get_barrier_semaphore()
-    greeted = [right, left, down, up] + x_peers + y_peers + z_peers + [core_peer]
+    greeted = col_peers + row_peers
     for peer in greeted:
         pl.semaphore_signal(barrier, inc=1, device_id=peer, device_id_type=MESH)
 
@@ -79,17 +73,38 @@
         hi[k, rows, cols] = high
         lo[k, rows, cols] = (value - high.astype(F32)).astype(BF16)
 
-    def strips(start, strip):
-        return pl.ds(pl.multiple_of(start + strip, 8), 64)
-
-    squares = jnp.zeros((8, B), F32)
-    for t in (PR, ML, ER, ZD):
+    sent = {}
+
+    def send(source, rxi, q, peer):
+        i, j = QUADS[q]
+        where = (pl.ds(i * B, B), pl.ds(j * B, B))
+        copy = pltpu.make_async_remote_copy(
+            src_ref=source(*where),
+            dst_ref=rx.at[(rxi,) + where],
+            send_sem=send_sem.at[rxi * 4 + q],
+            recv_sem=recv_sem.at[rxi * 4 + q],
+            device_id=peer,
+            device_id_type=MESH,
+        )
+        copy.start()
+        sent[rxi, q] = copy
+
+    def from_own(t):
+        return lambda rows, cols: own.at[t, rows, cols]
+
+    def from_rx(k):
+        return lambda rows, cols: rx.at[k, rows, cols]
+
+    def from_y(k):
+        return lambda rows, cols: y.at[k, rows, cols]
+
+    def own_blocks(t, squares):
         for q, (z, z2) in enumerate(QUADS):
             loads[t, q].wait()
             keep = mask[z, block_slot(t, z, z2) - 1].astype(F32)
             cols = pl.ds(z2 * B, B)
 
-            def strip_step(s, total, t=t, z=z, cols=cols, keep=keep):
+            def strip_step(s, total, z=z, cols=cols, keep=keep):
                 rows = pl.ds(pl.multiple_of(z * B + s * 64, 64), 64)
                 value = own[t, rows, cols] * keep
                 own[t, rows, cols] = value
@@ -97,6 +112,16 @@
                 return total + jnp.sum((value * value).reshape(8, 8, B), axis=0)
 
             squares = lax.fori_loop(0, 4, strip_step, squares)
+        return squares
+
+    squares = own_blocks(PR, jnp.zeros((8, B), F32))
+    squares = own_blocks(ML, squares)
+    pl.semaphore_wait(barrier, len(greeted))
+    for q in (0, 1):
+        send(from_own(PR), P_L, q, right)
+        send(from_own(ML), M_R, q, left)
+    squares = own_blocks(ER, squares)
+    squares = own_blocks(ZD, squares)
     squares = 2.0 * squares
     trace = jnp.zeros((8, B), F32)
     diag = lax.broadcasted_iota(jnp.int32, (B, B), 0) == lax.broadcasted_iota(jnp.int32, (B, B), 1)
@@ -121,8 +146,6 @@
     part[0, 0:8, :] = trace
     part[0, 8:16, :] = squares
 
-    pl.semaphore_wait(barrier, len(greeted))
-
     small = []
 
     def send_part(stage, peers, base):
@@ -148,31 +171,6 @@
             total = total + gath[base + n]
         part[stage + 1] = total
 
-    sent = {}
-
-    def send(source, rxi, q, peer):
-        i, j = QUADS[q]
-        where = (pl.ds(i * B, B), pl.ds(j * B, B))
-        copy = pltpu.make_async_remote_copy(
-            src_ref=source(*where),
-            dst_ref=rx.at[(rxi,) + where],
-            send_sem=send_sem.at[rxi * 4 + q],
-            recv_sem=recv_sem.at[rxi * 4 + q],
-            device_id=peer,
-            device_id_type=MESH,
-        )
-        copy.start()
-        sent[rxi, q] = copy
-
-    def from_own(t):
-        return lambda rows, cols: own.at[t, rows, cols]
-
-    def from_rx(k):
-        return lambda rows, cols: rx.at[k, rows, cols]
-
-    def from_y(k):
-        return lambda rows, cols: y.at[k, rows, cols]
-
     def prep(rxi, q, flip=False, keep=True):
         i, j = QUADS[q]
 
@@ -202,13 +200,7 @@
             take(rxi, (q,), forward, flip=q == 1)
 
     def products(yi, terms, first=False):
-        def tile(step, carry):
-            if yi == DG:
-                m, n = step // 2, (step + 1) // 2
-            else:
-                m, n = step // 2, step % 2
-            rows = pl.ds(pl.multiple_of(m * B, B), B)
-            cols = pl.ds(pl.multiple_of(n * B, B), B)
+        def tile(rows, cols):
             total = None if first else y[yi, rows, cols]
             for a, b, turned in terms:
                 a_hi = hi[a, rows, :]
@@ -223,9 +215,17 @@
                     term = lax.dot_general(u, v, dims, preferred_element_type=F32)
                     total = term if total is None else total + term
             y[yi, rows, cols] = total
-            return carry
-
-        lax.fori_loop(0, 3 if yi == DG else 4, tile, 0)
+
+        if yi == DG:
+            tile(top, top)
+            tile(slice(None), low)
+        else:
+
+            def column(n, carry):
+                tile(slice(None), pl.ds(pl.multiple_of(n * B, B), B))
+                return carry
+
+            lax.fori_loop(0, 2, column, 0)
 
     outs = []
 
@@ -262,15 +262,21 @@
             copy.start()
             outs.append(copy)
 
-    x_parts = send_part(0, x_peers, 0)
-    for q in range(4):
+    col_parts = send_part(0, col_peers, 0)
+
+    for q in (2, 3):
         send(from_own(PR), P_L, q, right)
         send(from_own(ML), M_R, q, left)
     for q in range(4):
         send(from_own(ER), E_L, q, right)
         send(from_own(ZD), Z_R, q, left)
+        send(from_own(ZD), Z_U, q, down)
+        send(from_own(ER), E_W, q, up)
     for q in DQUADS:
         send(from_own(DG), D_R, q, left)
+        send(from_own(DG), D_W, q, up)
+    for q in range(4):
+        send(from_own(PR), P_U, q, down)
 
     for z, slots in ((0, (2, 5, 8, 11)), (1, (1, 4, 7, 10, 13))):
         for slot in slots:
@@ -278,46 +284,22 @@
             copy.start()
             outs.append(copy)
 
-    products(ER, [(DG, ER, False)], first=True)
-    add_parts(0, x_parts, 0)
-    z_parts = send_part(1, z_peers, 3)
-
-    for q in range(4):
-        send(from_own(ZD), Z_U, q, down)
-        send(from_own(ER), E_W, q, up)
-    for q in DQUADS:
-        send(from_own(DG), D_W, q, up)
-    for q in range(4):
-        send(from_own(PR), P_U, q, down)
-
     for q, (i, j) in enumerate(QUADS):
         value = own[ER, pl.ds(i * B, B), pl.ds(j * B, B)].T
         put_split(ET, pl.ds(j * B, B), pl.ds(i * B, B), value)
 
     products(QQ, [(ET, ZD, False)], first=True)
-    add_parts(1, z_parts, 3)
-    y_parts = send_part(2, y_peers, 6)
-    products(DG, [(DG, DG, False), (ER, ER, True), (ML, ML, True)], first=True)
-    add_parts(2, y_parts, 6)
-    core_part = send_part(3, [core_peer], 9)
-
+    products(ER, [(DG, ER, False)], first=True)
     take(P_L, (0,), (P_UL, down))
     take(M_R, (0,), (M_UR, down))
-    products(DG, [(ZD, ZD, True), (PR, PR, True)])
-    core_part[0].wait_recv()
-    total = part[3] + gath[9]
-    t1 = jnp.sum(total[0:8, :])
-    t2 = jnp.sum(total[8:16, :])
-    goal = float(nrow * ncol * B)
-    lean = (jnp.abs(t2 - goal) - jnp.abs(2.0 * t1 - t2 - goal)) / B
-    steer[...] = 2.0 / (1.0 + jnp.exp(-jnp.full((8, B), lean, F32)))
-
+    products(DG, [(DG, DG, False), (ER, ER, True), (ML, ML, True), (ZD, ZD, True), (PR, PR, True)], first=True)
     take(P_L, (1,), (P_UL, down))
     take(M_R, (1,), (M_UR, down))
     products(ML, [(DG, ML, False)], first=True)
-    products(ZD, [(DG, ZD, False)], first=True)
     take(P_L, (2,), (P_UL, down))
     take(M_R, (2,), (M_UR, down))
+    add_parts(0, col_parts, 0)
+    row_parts = send_part(1, row_peers, 15)
     products(PR, [(DG, PR, False)], first=True)
     take_d(D_W)
     take(P_L, (3,), (P_UL, down))
@@ -331,7 +313,7 @@
     take(P_U)
     take_t(E_L, (0,), (E_WL, up))
     take(Z_R, (0,), (Z_UR, down))
-    products(ZD, [(ZD, sp(D_W), False), (ER, sp(M_R), False), (PR, sp(E_W), True)])
+    products(ZD, [(DG, ZD, False), (ZD, sp(D_W), False), (ER, sp(M_R), False), (PR, sp(E_W), True)], first=True)
     take_t(E_L, (1,), (E_WL, up))
     take(Z_R, (1,), (Z_UR, down))
     products(ER, [(ZD, sp(M_R), True), (sp(Z_U), sp(P_U), False)])
@@ -350,6 +332,13 @@
     take_d(D_R, (1,), (D_WR, up))
     products(DG, [(sp(E_L), sp(E_L), True), (sp(P_UL), sp(P_UL), True), (sp(M_UR), sp(M_UR), True)])
     take_d(D_R, (3,), (D_WR, up))
+    add_parts(1, row_parts, 15)
+    total = part[2]
+    t1 = jnp.sum(total[0:8, :])
+    t2 = jnp.sum(total[8:16, :])
+    goal = float(nrow * ncol * B)
+    lean = (jnp.abs(t2 - goal) - jnp.abs(2.0 * t1 - t2 - goal)) / B
+    steer[...] = 2.0 / (1.0 + jnp.exp(-jnp.full((8, B), lean, F32)))
     finish(DG)
     take(Z_UR)
     products(ER, [(ER, sp(D_R), False), (sp(M_UR), sp(Z_UR), False)])
@@ -389,15 +378,15 @@
             pltpu.VMEM((6 + NRX, W2, W2), BF16),
             pltpu.VMEM((6, W2, W2), F32),
             pltpu.VMEM((B, B), F32),
-            pltpu.VMEM((4, 16, B), F32),
-            pltpu.VMEM((10, 16, B), F32),
+            pltpu.VMEM((3, 16, B), F32),
+            pltpu.VMEM((22, 16, B), F32),
             pltpu.VMEM((8, B), F32),
             pltpu.SemaphoreType.DMA((19,)),
             pltpu.SemaphoreType.DMA((28,)),
             pltpu.SemaphoreType.DMA((NRX * 4,)),
             pltpu.SemaphoreType.DMA((NRX * 4,)),
-            pltpu.SemaphoreType.DMA((10,)),
-            pltpu.SemaphoreType.DMA((10,)),
+            pltpu.SemaphoreType.DMA((22,)),
+            pltpu.SemaphoreType.DMA((22,)),
         ],
         compiler_params=pltpu.CompilerParams(
             collective_id=0, has_side_effects=True, vmem_limit_bytes=62 * 1024 * 1024

time: 127 us -> 91.9 us (0.72)
  the two profiles are of different devices: /device:TPU:30 before, /device:TPU:0 now
where the time goes in v2:
time: 91.9 us; the launch traced here: 91.4 us
  Pallas kernels  84.4 us (92%)
  local copies, waits for them, and re-layouts  6.93 us (8%)
    pallas_call x1, Pallas kernels, shards(): pl.pallas_call(kernel, out_shape=jax.ShapeDtypeStruct(shape[2:], F32), in...  84.4 us
    unnamed x1, local copies, waits for them, and re-layouts  6.93 us

profile of v2, /device:TPU:0, one launch (start us, length us, event | category | flops | bytes accessed | tf_op | source)
XLA Modules:
  0.0 91.4 jit_solution(5048900946420302940)
XLA Ops:
  0.0 84.4 %sp2_step.1 = f32[2,14,256,256]{3,2,1,0:T(8,128)} custom-call(f32[2,14,256,256]{3,2,1,0:T(8,128)} %bitcast.5, f32[2,256]{1,0:T(2,128)} %bitcast.6, s32[2,13]{1,0:T(2,128)} %bitcast.7), custom_call_target="tpu_custom_call" | custom-call | tf_op jit(solution)/shard_map/sp2_step/pallas_call | solution.py:365
  84.4 6.9 %copy.5 = f32[1,1,2,14,256,256]{5,4,3,2,1,0:T(8,128)} copy(f32[1,1,2,14,256,256]{5,4,3,2,1,0:T(8,128)} %bitcast.4) | data formatting | bytes 14680064

commit v3 on v2

--- a/solution.py
+++ b/solution.py
@@ -32,8 +32,8 @@
     return MIDDLE[t] + z2 - z
 
 
-def kernel(stored, onsite, mask, out, own, rx, hi, lo, y, zero, part, gath, steer,
-           in_sem, out_sem, send_sem, recv_sem, ar_send, ar_recv):
+def kernel(stored, onsite, mask, y, own, rx, hi, lo, handed, part, gath, steer,
+           in_sem, send_sem, recv_sem, ar_send, ar_recv):
     row = lax.axis_index("row")
     col = lax.axis_index("col")
     nrow = lax.axis_size("row")
@@ -46,13 +46,15 @@
     row_peers = [(lax.rem(row + j, nrow), col) for j in range(1, nrow)]
 
     loads = {}
-    for t in (PR, ML, ER, ZD):
-        for q, (z, z2) in enumerate(QUADS):
-            loads[t, q] = pltpu.make_async_copy(
-                stored.at[z, block_slot(t, z, z2)],
-                own.at[t, pl.ds(z * B, B), pl.ds(z2 * B, B)],
-                in_sem.at[(t - 1) * 4 + q],
-            )
+    for t, q in [(t, q) for q in range(4) for t in (PR, ML)] + [
+        (t, q) for t in (ER, ZD) for q in range(4)
+    ]:
+        z, z2 = QUADS[q]
+        loads[t, q] = pltpu.make_async_copy(
+            stored.at[z, block_slot(t, z, z2)],
+            own.at[t, pl.ds(z * B, B), pl.ds(z2 * B, B)],
+            in_sem.at[(t - 1) * 4 + q],
+        )
     for n, (q, z, slot) in enumerate(((0, 0, 0), (1, 0, 1), (3, 1, 0))):
         i, j = QUADS[q]
         loads[DG, q] = pltpu.make_async_copy(
@@ -65,8 +67,6 @@
     greeted = col_peers + row_peers
     for peer in greeted:
         pl.semaphore_signal(barrier, inc=1, device_id=peer, device_id_type=MESH)
-
-    zero[...] = jnp.zeros_like(zero)
 
     def put_split(k, rows, cols, value):
         high = value.astype(BF16)
@@ -95,33 +95,36 @@
     def from_rx(k):
         return lambda rows, cols: rx.at[k, rows, cols]
 
-    def from_y(k):
-        return lambda rows, cols: y.at[k, rows, cols]
-
-    def own_blocks(t, squares):
-        for q, (z, z2) in enumerate(QUADS):
-            loads[t, q].wait()
-            keep = mask[z, block_slot(t, z, z2) - 1].astype(F32)
-            cols = pl.ds(z2 * B, B)
-
-            def strip_step(s, total, z=z, cols=cols, keep=keep):
-                rows = pl.ds(pl.multiple_of(z * B + s * 64, 64), 64)
-                value = own[t, rows, cols] * keep
-                own[t, rows, cols] = value
-                put_split(t, rows, cols, value)
-                return total + jnp.sum((value * value).reshape(8, 8, B), axis=0)
-
-            squares = lax.fori_loop(0, 4, strip_step, squares)
-        return squares
-
-    squares = own_blocks(PR, jnp.zeros((8, B), F32))
-    squares = own_blocks(ML, squares)
-    pl.semaphore_wait(barrier, len(greeted))
-    for q in (0, 1):
-        send(from_own(PR), P_L, q, right)
-        send(from_own(ML), M_R, q, left)
-    squares = own_blocks(ER, squares)
-    squares = own_blocks(ZD, squares)
+    def from_handed(rows, cols):
+        return handed.at[0, rows, cols]
+
+    def own_block(t, q, squares):
+        z, z2 = QUADS[q]
+        loads[t, q].wait()
+        keep = mask[z, block_slot(t, z, z2) - 1].astype(F32)
+        cols = pl.ds(z2 * B, B)
+
+        def strip_step(s, total):
+            rows = pl.ds(pl.multiple_of(z * B + s * 64, 64), 64)
+            value = own[t, rows, cols] * keep
+            own[t, rows, cols] = value
+            put_split(t, rows, cols, value)
+            return total + jnp.sum((value * value).reshape(8, 8, B), axis=0)
+
+        return lax.fori_loop(0, 4, strip_step, squares)
+
+    squares = jnp.zeros((8, B), F32)
+    for q in range(4):
+        squares = own_block(PR, q, squares)
+        squares = own_block(ML, q, squares)
+        if q == 0:
+            pl.semaphore_wait(barrier, len(greeted))
+        if q < 2:
+            send(from_own(PR), P_L, q, right)
+            send(from_own(ML), M_R, q, left)
+    for t in (ER, ZD):
+        for q in range(4):
+            squares = own_block(t, q, squares)
     squares = 2.0 * squares
     trace = jnp.zeros((8, B), F32)
     diag = lax.broadcasted_iota(jnp.int32, (B, B), 0) == lax.broadcasted_iota(jnp.int32, (B, B), 1)
@@ -143,8 +146,10 @@
     flipped = value.T
     own[DG, low, top] = flipped
     put_split(DG, low, top, flipped)
-    part[0, 0:8, :] = trace
-    part[0, 8:16, :] = squares
+    trace = trace[:, :128] + trace[:, 128:]
+    squares = squares[:, :128] + squares[:, 128:]
+    part[0, 0:4, :] = trace[0:4] + trace[4:8]
+    part[0, 4:8, :] = squares[0:4] + squares[4:8]
 
     small = []
 
@@ -200,8 +205,10 @@
             take(rxi, (q,), forward, flip=q == 1)
 
     def products(yi, terms, first=False):
+        held, slot = (handed, 0) if yi == QQ else (y, yi)
+
         def tile(rows, cols):
-            total = None if first else y[yi, rows, cols]
+            total = None if first else held[slot, rows, cols]
             for a, b, turned in terms:
                 a_hi = hi[a, rows, :]
                 a_lo = lo[a, rows, :]
@@ -214,7 +221,7 @@
                 for u, v in ((a_hi, b_hi), (a_hi, b_lo), (a_lo, b_hi)):
                     term = lax.dot_general(u, v, dims, preferred_element_type=F32)
                     total = term if total is None else total + term
-            y[yi, rows, cols] = total
+            held[slot, rows, cols] = total
 
         if yi == DG:
             tile(top, top)
@@ -226,8 +233,6 @@
                 return carry
 
             lax.fori_loop(0, 2, column, 0)
-
-    outs = []
 
     def finish(yi, extra=None):
         quads = DQUADS if yi == DG else range(4)
@@ -254,13 +259,6 @@
                 return carry
 
             lax.fori_loop(0, 4, strip_step, 0)
-            copy = pltpu.make_async_copy(
-                y.at[yi, pl.ds(z * B, B), pl.ds(z2 * B, B)],
-                out.at[z, slot],
-                out_sem.at[z * 14 + slot],
-            )
-            copy.start()
-            outs.append(copy)
 
     col_parts = send_part(0, col_peers, 0)
 
@@ -277,12 +275,6 @@
         send(from_own(DG), D_W, q, up)
     for q in range(4):
         send(from_own(PR), P_U, q, down)
-
-    for z, slots in ((0, (2, 5, 8, 11)), (1, (1, 4, 7, 10, 13))):
-        for slot in slots:
-            copy = pltpu.make_async_copy(zero, out.at[z, slot], out_sem.at[z * 14 + slot])
-            copy.start()
-            outs.append(copy)
 
     for q, (i, j) in enumerate(QUADS):
         value = own[ER, pl.ds(i * B, B), pl.ds(j * B, B)].T
@@ -306,7 +298,7 @@
     take(M_R, (3,), (M_UR, down))
     products(QQ, [(sp(M_R), sp(D_W), False)])
     for q in range(4):
-        send(from_y(QQ), Q_L, q, right)
+        send(from_handed, Q_L, q, right)
 
     take(E_W)
     take_t(Z_U)
@@ -334,8 +326,8 @@
     take_d(D_R, (3,), (D_WR, up))
     add_parts(1, row_parts, 15)
     total = part[2]
-    t1 = jnp.sum(total[0:8, :])
-    t2 = jnp.sum(total[8:16, :])
+    t1 = jnp.sum(total[0:4, :])
+    t2 = jnp.sum(total[4:8, :])
     goal = float(nrow * ncol * B)
     lean = (jnp.abs(t2 - goal) - jnp.abs(2.0 * t1 - t2 - goal)) / B
     steer[...] = 2.0 / (1.0 + jnp.exp(-jnp.full((8, B), lean, F32)))
@@ -352,47 +344,71 @@
     finish(PR)
     finish(ML, Q_L)
 
-    for copy in outs:
-        copy.wait()
     for copy in small:
         copy.wait_send()
     for copy in sent.values():
         copy.wait_send()
 
 
+def write(y, out, zero, sem):
+    zero[...] = jnp.zeros_like(zero)
+    copies = [(z, slot) for z in range(2) for slot in range(14)]
+    started = []
+    for t in range(5):
+        for q in DQUADS if t == DG else range(4):
+            z, z2 = QUADS[q]
+            slot = (1 if q == 1 else 0) if t == DG else block_slot(t, z, z2)
+            copies.remove((z, slot))
+            started.append((y.at[t, pl.ds(z * B, B), pl.ds(z2 * B, B)], z, slot))
+    started = [
+        pltpu.make_async_copy(source, out.at[z, slot], sem.at[z * 14 + slot])
+        for source, z, slot in started + [(zero, z, slot) for z, slot in copies]
+    ]
+    for copy in started:
+        copy.start()
+    for copy in started:
+        copy.wait()
+
+
 def shards(stored_blocks, onsite, bond_mask):
-    shape = stored_blocks.shape
-    result = pl.pallas_call(
+    squared = pl.pallas_call(
         kernel,
-        out_shape=jax.ShapeDtypeStruct(shape[2:], F32),
+        out_shape=pltpu.VMEM((5, W2, W2), F32),
         in_specs=[
-            pl.BlockSpec(memory_space=pl.ANY),
+            pl.BlockSpec(memory_space=pltpu.HBM),
             pl.BlockSpec(memory_space=pltpu.VMEM),
             pl.BlockSpec(memory_space=pltpu.SMEM),
         ],
-        out_specs=pl.BlockSpec(memory_space=pl.ANY),
+        out_specs=pl.BlockSpec(memory_space=pltpu.VMEM),
         scratch_shapes=[
             pltpu.VMEM((5, W2, W2), F32),
             pltpu.VMEM((NRX, W2, W2), F32),
             pltpu.VMEM((6 + NRX, W2, W2), BF16),
             pltpu.VMEM((6 + NRX, W2, W2), BF16),
-            pltpu.VMEM((6, W2, W2), F32),
-            pltpu.VMEM((B, B), F32),
-            pltpu.VMEM((3, 16, B), F32),
-            pltpu.VMEM((22, 16, B), F32),
+            pltpu.VMEM((1, W2, W2), F32),
+            pltpu.VMEM((3, 8, 128), F32),
+            pltpu.VMEM((22, 8, 128), F32),
             pltpu.VMEM((8, B), F32),
             pltpu.SemaphoreType.DMA((19,)),
-            pltpu.SemaphoreType.DMA((28,)),
             pltpu.SemaphoreType.DMA((NRX * 4,)),
             pltpu.SemaphoreType.DMA((NRX * 4,)),
             pltpu.SemaphoreType.DMA((22,)),
             pltpu.SemaphoreType.DMA((22,)),
         ],
         compiler_params=pltpu.CompilerParams(
-            collective_id=0, has_side_effects=True, vmem_limit_bytes=62 * 1024 * 1024
+            collective_id=0, has_side_effects=True, vmem_limit_bytes=50 * 1024 * 1024
         ),
         name="sp2_step",
     )(stored_blocks[0, 0], onsite[0, 0], bond_mask[0, 0])
+    result = pl.pallas_call(
+        write,
+        out_shape=jax.ShapeDtypeStruct(stored_blocks.shape[2:], F32),
+        in_specs=[pl.BlockSpec(memory_space=pltpu.VMEM)],
+        out_specs=pl.BlockSpec(memory_space=pltpu.HBM),
+        scratch_shapes=[pltpu.VMEM((B, B), F32), pltpu.SemaphoreType.DMA((28,))],
+        compiler_params=pltpu.CompilerParams(vmem_limit_bytes=4 * 1024 * 1024),
+        name="write_out",
+    )(squared)
     return result[None, None]
 
 

time: 91.9 us -> 85.3 us (0.928)
  local copies, waits for them, and re-layouts: 6.93 us -> 0 us
    unnamed x1 -> x0, local copies, waits for them, and re-layouts: 6.93 us -> none
    pallas_call x1 -> x2, Pallas kernels: 84.4 us -> 84.5 us  [the longest x1 81.4 us: shards(): pl.pallas_call(kernel, out_shape=pltpu.VMEM((5, W2, W2), F32), in_specs=[...]
where the time goes in v3:
time: 85.3 us; the launch traced here: 84.7 us
  Pallas kernels  84.5 us (99%)
    pallas_call x1, Pallas kernels, shards(): pl.pallas_call(kernel, out_shape=pltpu.VMEM((5, W2, W2), F32), in_specs=[...  81.4 us
    pallas_call x1, Pallas kernels, shards(): pl.pallas_call(write, out_shape=jax.ShapeDtypeStruct(stored_blocks.shape[...  3.19 us

profile of v3, /device:TPU:0, one launch (start us, length us, event | category | flops | bytes accessed | tf_op | source)
XLA Modules:
  0.0 84.7 jit_solution(11855492226583394406)
XLA Ops:
  0.0 81.4 %sp2_step.1.y = f32[5,512,512]{2,1,0:T(8,128)S(1)} custom-call(f32[2,14,256,256]{3,2,1,0:T(8,128)} %bitcast.4, f32[2,256]{1,0:T(2,128)} %bitcast.5, s32[2,13]{1,0:T(2,128)} %bitcast.6), custom_call_target="tpu_custom_call" | custom-call | tf_op jit(solution)/shard_map/sp2_step/pallas_call | solution.py:374
  81.4 3.2 %write_out.1 = f32[2,14,256,256]{3,2,1,0:T(8,128)} custom-call(f32[5,512,512]{2,1,0:T(8,128)S(1)} %sp2_step.1.y), custom_call_target="tpu_custom_call" | custom-call | tf_op jit(solution)/shard_map/write_out/pallas_call | solution.py:403

commit v4 on v3

--- a/solution.py
+++ b/solution.py
@@ -32,8 +32,8 @@
     return MIDDLE[t] + z2 - z
 
 
-def kernel(stored, onsite, mask, y, own, rx, hi, lo, handed, part, gath, steer,
-           in_sem, send_sem, recv_sem, ar_send, ar_recv):
+def kernel(stored, onsite_in, mask_in, y, own, rx, hi, lo, handed, part, gath, steer, onsite, mask,
+           in_sem, send_sem, recv_sem, ar_send, ar_recv, round_sem):
     row = lax.axis_index("row")
     col = lax.axis_index("col")
     nrow = lax.axis_size("row")
@@ -45,6 +45,21 @@
     col_peers = [(row, lax.rem(col + j, ncol)) for j in range(1, ncol)]
     row_peers = [(lax.rem(row + j, nrow), col) for j in range(1, nrow)]
 
+    near = [(row, lax.rem(col + j, ncol)) for j in (1, ncol - 1, 4, ncol - 4)]
+    near += [(lax.rem(row + j, nrow), col) for j in (1, nrow - 1, 2, nrow - 2)]
+    barrier = pltpu.get_barrier_semaphore()
+
+    def tell(sem):
+        for peer in near:
+            pl.semaphore_signal(sem, inc=1, device_id=peer, device_id_type=MESH)
+
+    def heard(sem):
+        pl.semaphore_wait(sem, len(near))
+
+    tell(barrier)
+
+    mask_load = pltpu.make_async_copy(mask_in, mask, in_sem.at[19])
+    mask_load.start()
     loads = {}
     for t, q in [(t, q) for q in range(4) for t in (PR, ML)] + [
         (t, q) for t in (ER, ZD) for q in range(4)
@@ -63,10 +78,9 @@
     for copy in loads.values():
         copy.start()
 
-    barrier = pltpu.get_barrier_semaphore()
-    greeted = col_peers + row_peers
-    for peer in greeted:
-        pl.semaphore_signal(barrier, inc=1, device_id=peer, device_id_type=MESH)
+    onsite_load = pltpu.make_async_copy(onsite_in, onsite, in_sem.at[20])
+    onsite_load.start()
+    mask_load.wait()
 
     def put_split(k, rows, cols, value):
         high = value.astype(BF16)
@@ -113,20 +127,25 @@
 
         return lax.fori_loop(0, 4, strip_step, squares)
 
-    squares = jnp.zeros((8, B), F32)
+    squares = own_block(PR, 0, jnp.zeros((8, B), F32))
+    heard(barrier)
+    send(from_own(PR), P_L, 0, right)
+    tell(round_sem.at[0])
+    squares = own_block(ML, 0, squares)
+    send(from_own(ML), M_R, 0, left)
+    squares = own_block(PR, 1, squares)
+    send(from_own(PR), P_L, 1, right)
+    squares = own_block(ML, 1, squares)
+    send(from_own(ML), M_R, 1, left)
+    for t, q in [(t, q) for q in (2, 3) for t in (PR, ML)] + [(ER, q) for q in range(4)]:
+        squares = own_block(t, q, squares)
+    heard(round_sem.at[0])
+    tell(round_sem.at[1])
     for q in range(4):
-        squares = own_block(PR, q, squares)
-        squares = own_block(ML, q, squares)
-        if q == 0:
-            pl.semaphore_wait(barrier, len(greeted))
-        if q < 2:
-            send(from_own(PR), P_L, q, right)
-            send(from_own(ML), M_R, q, left)
-    for t in (ER, ZD):
-        for q in range(4):
-            squares = own_block(t, q, squares)
+        squares = own_block(ZD, q, squares)
     squares = 2.0 * squares
     trace = jnp.zeros((8, B), F32)
+    onsite_load.wait()
     diag = lax.broadcasted_iota(jnp.int32, (B, B), 0) == lax.broadcasted_iota(jnp.int32, (B, B), 1)
     for z, q in ((0, 0), (1, 3)):
         loads[DG, q].wait()
@@ -204,7 +223,7 @@
         for q in quads:
             take(rxi, (q,), forward, flip=q == 1)
 
-    def products(yi, terms, first=False):
+    def products(yi, terms, first=False, column=None):
         held, slot = (handed, 0) if yi == QQ else (y, yi)
 
         def tile(rows, cols):
@@ -226,16 +245,18 @@
         if yi == DG:
             tile(top, top)
             tile(slice(None), low)
+        elif column is not None:
+            tile(slice(None), pl.ds(column * B, B))
         else:
 
-            def column(n, carry):
+            def each(n, carry):
                 tile(slice(None), pl.ds(pl.multiple_of(n * B, B), B))
                 return carry
 
-            lax.fori_loop(0, 2, column, 0)
-
-    def finish(yi, extra=None):
-        quads = DQUADS if yi == DG else range(4)
+            lax.fori_loop(0, 2, each, 0)
+
+    def finish(yi, extra=None, quads=range(4)):
+        quads = DQUADS if yi == DG else quads
         for q in quads:
             z, z2 = QUADS[q]
             if yi == DG:
@@ -260,6 +281,7 @@
 
             lax.fori_loop(0, 4, strip_step, 0)
 
+    heard(round_sem.at[1])
     col_parts = send_part(0, col_peers, 0)
 
     for q in (2, 3):
@@ -317,13 +339,11 @@
     take(Z_R, (3,), (Z_UR, down))
     products(ZD, [(sp(E_L), sp(P_L), False)])
     products(ER, [(PR, sp(Z_R), True)])
+    take_d(D_R, (0,), (D_WR, up))
+    products(PR, [(ER, sp(Z_R), False)])
     take_t(P_UL)
     take_t(M_UR)
-    take_d(D_R, (0,), (D_WR, up))
-    products(PR, [(ER, sp(Z_R), False)])
-    take_d(D_R, (1,), (D_WR, up))
     products(DG, [(sp(E_L), sp(E_L), True), (sp(P_UL), sp(P_UL), True), (sp(M_UR), sp(M_UR), True)])
-    take_d(D_R, (3,), (D_WR, up))
     add_parts(1, row_parts, 15)
     total = part[2]
     t1 = jnp.sum(total[0:4, :])
@@ -331,18 +351,28 @@
     goal = float(nrow * ncol * B)
     lean = (jnp.abs(t2 - goal) - jnp.abs(2.0 * t1 - t2 - goal)) / B
     steer[...] = 2.0 / (1.0 + jnp.exp(-jnp.full((8, B), lean, F32)))
+    take_d(D_R, (1,), (D_WR, up))
+    products(ER, [(ER, sp(D_R), False)], column=0)
     finish(DG)
-    take(Z_UR)
-    products(ER, [(ER, sp(D_R), False), (sp(M_UR), sp(Z_UR), False)])
-    finish(ER)
     take(E_WL)
     products(ZD, [(ML, sp(E_WL), False)])
+    products(ML, [(ZD, sp(E_WL), True)])
+    take(Z_UR)
+    products(ER, [(sp(M_UR), sp(Z_UR), False)])
     finish(ZD)
-    products(ML, [(ZD, sp(E_WL), True)])
-    take_d(D_WR)
-    products(PR, [(PR, sp(D_WR), False)])
-    finish(PR)
-    finish(ML, Q_L)
+    finish(ER, quads=(0, 2))
+    finish(ML, Q_L, (0, 1))
+    take_d(D_R, (3,), (D_WR, up))
+    products(ER, [(ER, sp(D_R), False)], column=1)
+    finish(ER, quads=(1, 3))
+    take_d(D_WR, (0, 1))
+    products(PR, [(PR, sp(D_WR), False)], column=0)
+    finish(PR, quads=(0, 2))
+    finish(ML, Q_L, (2,))
+    take_d(D_WR, (3,))
+    products(PR, [(PR, sp(D_WR), False)], column=1)
+    finish(PR, quads=(1, 3))
+    finish(ML, Q_L, (3,))
 
     for copy in small:
         copy.wait_send()
@@ -376,8 +406,8 @@
         out_shape=pltpu.VMEM((5, W2, W2), F32),
         in_specs=[
             pl.BlockSpec(memory_space=pltpu.HBM),
-            pl.BlockSpec(memory_space=pltpu.VMEM),
-            pl.BlockSpec(memory_space=pltpu.SMEM),
+            pl.BlockSpec(memory_space=pltpu.HBM),
+            pl.BlockSpec(memory_space=pltpu.HBM),
         ],
         out_specs=pl.BlockSpec(memory_space=pltpu.VMEM),
         scratch_shapes=[
@@ -389,11 +419,14 @@
             pltpu.VMEM((3, 8, 128), F32),
             pltpu.VMEM((22, 8, 128), F32),
             pltpu.VMEM((8, B), F32),
-            pltpu.SemaphoreType.DMA((19,)),
+            pltpu.VMEM((2, B), F32),
+            pltpu.SMEM((2, 13), jnp.int32),
+            pltpu.SemaphoreType.DMA((21,)),
             pltpu.SemaphoreType.DMA((NRX * 4,)),
             pltpu.SemaphoreType.DMA((NRX * 4,)),
             pltpu.SemaphoreType.DMA((22,)),
             pltpu.SemaphoreType.DMA((22,)),
+            pltpu.SemaphoreType.REGULAR((2,)),
         ],
         compiler_params=pltpu.CompilerParams(
             collective_id=0, has_side_effects=True, vmem_limit_bytes=50 * 1024 * 1024

time: 85.3 us -> 83.3 us (0.977)
  Pallas kernels: 84.5 us -> 83 us
    pallas_call x1, Pallas kernels: 81.4 us -> 79.8 us  [shards(): pl.pallas_call(kernel, out_shape=pltpu.VMEM((5, W2, W2), F32), in_specs=[...]
where the time goes in v4:
time: 83.3 us; the launch traced here: 83.2 us
  Pallas kernels  83 us (100%)
    pallas_call x1, Pallas kernels, shards(): pl.pallas_call(kernel, out_shape=pltpu.VMEM((5, W2, W2), F32), in_specs=[...  79.8 us
    pallas_call x1, Pallas kernels, shards(): pl.pallas_call(write, out_shape=jax.ShapeDtypeStruct(stored_blocks.shape[...  3.19 us

profile of v4, /device:TPU:0, one launch (start us, length us, event | category | flops | bytes accessed | tf_op | source)
XLA Modules:
  0.0 83.2 jit_solution(710989847788253933)
XLA Ops:
  0.0 79.8 %sp2_step.1.y = f32[5,512,512]{2,1,0:T(8,128)S(1)} custom-call(f32[2,14,256,256]{3,2,1,0:T(8,128)} %bitcast.4, f32[2,256]{1,0:T(2,128)} %bitcast.5, s32[2,13]{1,0:T(2,128)} %bitcast.6), custom_call_target="tpu_custom_call" | custom-call | tf_op jit(solution)/shard_map/sp2_step/pallas_call | solution.py:404
  79.9 3.2 %write_out.1 = f32[2,14,256,256]{3,2,1,0:T(8,128)} custom-call(f32[5,512,512]{2,1,0:T(8,128)S(1)} %sp2_step.1.y), custom_call_target="tpu_custom_call" | custom-call | tf_op jit(solution)/shard_map/write_out/pallas_call | solution.py:436

commit v5 on v4

v5 whole, which is shorter than its diff:
```python
import jax
import jax.numpy as jnp
from jax import lax
from jax.experimental import pallas as pl
from jax.experimental.pallas import tpu as pltpu
from jax.sharding import PartitionSpec as P

MESH = pl.DeviceIdType.MESH
F32 = jnp.float32
BF16 = jnp.bfloat16
B = 256
W2 = 2 * B

DG, ER, ML, ZD, PR = range(5)
MIDDLE = {ER: 3, ML: 6, ZD: 9, PR: 12}
DP, ZP, QQ = range(3)

(DP_L, ZP_L, Q_L, M_R, Z_R, D_R, Z_U, P_U, M_UR, Z_UR, E_W, D_W, D_WR) = range(13)
NRX = 13
ET, P_UT = 5, 6


def sp(rx):
    return 4 + rx


NSPLIT = 4 + NRX

QUADS = ((0, 0), (0, 1), (1, 0), (1, 1))
DQUADS = (0, 1, 3)
SYM = {
    0: ((0, 0, 128, 0, 256), (1, 128, 128, 128, 128)),
    1: ((2, 0, 256, 256, 256),),
    3: ((3, 256, 128, 256, 256), (4, 384, 128, 384, 128)),
}


def block_slot(t, z, z2):
    return MIDDLE[t] + z2 - z


def kernel(stored, onsite_in, mask_in, y, own, rx, hi, lo, handed, part, gath, steer, onsite, mask,
           in_sem, send_sem, recv_sem, ar_send, ar_recv, round_sem):
    row = lax.axis_index("row")
    col = lax.axis_index("col")
    nrow = lax.axis_size("row")
    ncol = lax.axis_size("col")
    right = (row, lax.rem(col + 1, ncol))
    left = (row, lax.rem(col + ncol - 1, ncol))
    down = (lax.rem(row + 1, nrow), col)
    up = (lax.rem(row + nrow - 1, nrow), col)
    col_peers = [(row, lax.rem(col + j, ncol)) for j in range(1, ncol)]
    row_peers = [(lax.rem(row + j, nrow), col) for j in range(1, nrow)]

    near = [(row, lax.rem(col + j, ncol)) for j in (1, ncol - 1, 4, ncol - 4)]
    near += [(lax.rem(row + j, nrow), col) for j in (1, nrow - 1, 2, nrow - 2)]
    barrier = pltpu.get_barrier_semaphore()

    def tell(sem):
        for peer in near:
            pl.semaphore_signal(sem, inc=1, device_id=peer, device_id_type=MESH)

    def heard(sem):
        pl.semaphore_wait(sem, len(near))

    tell(barrier)

    mask_load = pltpu.make_async_copy(mask_in, mask, in_sem.at[19])
    mask_load.start()
    loads = {}
    for t, q in [(t, q) for q in range(4) for t in (PR, ML)] + [
        (t, q) for t in (ER, ZD) for q in range(4)
    ]:
        z, z2 = QUADS[q]
        loads[t, q] = pltpu.make_async_copy(
            stored.at[z, block_slot(t, z, z2)],
            own.at[t, pl.ds(z * B, B), pl.ds(z2 * B, B)],
            in_sem.at[(t - 1) * 4 + q],
        )
    for n, (q, z, slot) in enumerate(((0, 0, 0), (1, 0, 1), (3, 1, 0))):
        i, j = QUADS[q]
        loads[DG, q] = pltpu.make_async_copy(
            stored.at[z, slot], own.at[DG, pl.ds(i * B, B), pl.ds(j * B, B)], in_sem.at[16 + n]
        )
    for copy in loads.values():
        copy.start()

    onsite_load = pltpu.make_async_copy(onsite_in, onsite, in_sem.at[20])
    onsite_load.start()
    mask_load.wait()

    def put_split(k, rows, cols, value):
        high = value.astype(BF16)
        hi[k, rows, cols] = high
        lo[k, rows, cols] = (value - high.astype(F32)).astype(BF16)

    sent = {}

    def send_piece(source, rxi, p, where, peer):
        copy = pltpu.make_async_remote_copy(
            src_ref=source(*where),
            dst_ref=rx.at[(rxi,) + where],
            send_sem=send_sem.at[rxi * 5 + p],
            recv_sem=recv_sem.at[rxi * 5 + p],
            device_id=peer,
            device_id_type=MESH,
        )
        copy.start()
        sent[rxi, p] = copy

    def send(source, rxi, q, peer):
        i, j = QUADS[q]
        send_piece(source, rxi, q, (pl.ds(i * B, B), pl.ds(j * B, B)), peer)

    def send_sym(source, rxi, q, peer):
        for p, r, nr, c, nc in SYM[q]:
            send_piece(source, rxi, p, (pl.ds(r, nr), pl.ds(c, nc)), peer)

    def arrive_sym(rxi, q, forward=None):
        for p, r, nr, c, nc in SYM[q]:
            sent[rxi, p].wait_recv()
            if forward is not None:
                send_piece(from_rx(rxi), forward[0], p, (pl.ds(r, nr), pl.ds(c, nc)), forward[1])
        if q != 1:
            o = 0 if q == 0 else B
            mirrored = rx[rxi, pl.ds(o, 128), pl.ds(o + 128, 128)].T
            rx[rxi, pl.ds(o + 128, 128), pl.ds(o, 128)] = mirrored

    def from_own(t):
        return lambda rows, cols: own.at[t, rows, cols]

    def from_rx(k):
        return lambda rows, cols: rx.at[k, rows, cols]

    def from_handed(k):
        return lambda rows, cols: handed.at[k, rows, cols]

    def own_block(t, q, squares):
        z, z2 = QUADS[q]
        loads[t, q].wait()
        keep = mask[z, block_slot(t, z, z2) - 1].astype(F32)
        cols = pl.ds(z2 * B, B)

        def strip_step(s, total):
            rows = pl.ds(pl.multiple_of(z * B + s * 64, 64), 64)
            value = own[t, rows, cols] * keep
            own[t, rows, cols] = value
            put_split(t, rows, cols, value)
            return total + jnp.sum((value * value).reshape(8, 8, B), axis=0)

        return lax.fori_loop(0, 4, strip_step, squares)

    def prep(rxi, q, flip=None, keep=True):
        i, j = QUADS[q]

        def strip_step(s, carry):
            offset = pl.multiple_of(s * 128, 128)
            value = rx[rxi, pl.ds(i * B + offset, 128), pl.ds(j * B, B)]
            if keep:
                put_split(sp(rxi), pl.ds(i * B + offset, 128), pl.ds(j * B, B), value)
            if flip is not None:
                put_split(flip, pl.ds(j * B, B), pl.ds(i * B + offset, 128), value.T)
            return carry

        lax.fori_loop(0, 2, strip_step, 0)

    def take(rxi, quads=range(4), forward=None, **how):
        for q in quads:
            sent[rxi, q].wait_recv()
            if forward is not None:
                send(from_rx(rxi), forward[0], q, forward[1])
            prep(rxi, q, **how)

    def take_t(rxi, quads=range(4), forward=None):
        take(rxi, quads, forward, flip=sp(rxi), keep=False)

    def take_d(rxi, quads=DQUADS, forward=None):
        for q in quads:
            arrive_sym(rxi, q, forward)
            prep(rxi, q, flip=sp(rxi) if q == 1 else None)

    full = slice(None)

    def products(target, slot, terms, first=False, tiles=None):
        def tile(rows, cols):
            total = None if first else target[slot, rows, cols]
            for a, b, turned in terms:
                a_hi = hi[a, rows, :]
                a_lo = lo[a, rows, :]
                if turned:
                    b_hi, b_lo = hi[b, cols, :], lo[b, cols, :]
                    dims = (((1,), (1,)), ((), ()))
                else:
                    b_hi, b_lo = hi[b, :, cols], lo[b, :, cols]
                    dims = (((1,), (0,)), ((), ()))
                for u, v in ((a_hi, b_hi), (a_hi, b_lo), (a_lo, b_hi)):
                    term = lax.dot_general(u, v, dims, preferred_element_type=F32)
                    total = term if total is None else total + term
            target[slot, rows, cols] = total

        if tiles is not None:
            for rows, cols in tiles:
                tile(rows, cols)
        else:

            def each(n, carry):
                tile(full, pl.ds(pl.multiple_of(n * B, B), B))
                return carry

            lax.fori_loop(0, 2, each, 0)

    def finish(yi, extra=None, quads=range(4)):
        quads = DQUADS if yi == DG else quads
        for q in quads:
            z, z2 = QUADS[q]
            if yi == DG:
                slot = 1 if q == 1 else 0
            else:
                slot = block_slot(yi, z, z2)
            if extra is not None and yi == DG:
                arrive_sym(extra, q)
            elif extra is not None:
                sent[extra, q].wait_recv()
            keep = mask[z, slot - 1].astype(F32) if slot else None

            def strip_step(s, carry, z=z, z2=z2, keep=keep):
                rows = pl.ds(pl.multiple_of(z * B + s * 64, 64), 64)
                cols = pl.ds(z2 * B, B)
                value = y[yi, rows, cols]
                if extra is not None:
                    value = value + rx[extra, rows, cols]
                value = value + steer[0:1, :] * (own[yi, rows, cols] - value)
                if keep is not None:
                    value = value * keep
                y[yi, rows, cols] = value
                return carry

            lax.fori_loop(0, 4, strip_step, 0)

    top, low = pl.ds(0, B), pl.ds(B, B)
    squares = own_block(PR, 0, jnp.zeros((8, B), F32))
    heard(barrier)
    send(from_own(PR), P_U, 0, down)
    tell(round_sem.at[0])
    squares = own_block(ML, 0, squares)
    send(from_own(ML), M_R, 0, left)
    squares = own_block(PR, 2, squares)
    send(from_own(PR), P_U, 2, down)
    for p, m in ((1, 1), (3, 2)):
        squares = own_block(PR, p, squares)
        send(from_own(PR), P_U, p, down)
        squares = own_block(ML, m, squares)
        send(from_own(ML), M_R, m, left)
    squares = own_block(ML, 3, squares)
    for q in range(4):
        squares = own_block(ER, q, squares)
    send(from_own(ML), M_R, 3, left)
    for q, (i, j) in enumerate(QUADS):
        send(from_own(ER), E_W, q, up)
        value = own[ER, pl.ds(i * B, B), pl.ds(j * B, B)].T
        put_split(ET, pl.ds(j * B, B), pl.ds(i * B, B), value)
    heard(round_sem.at[0])
    tell(round_sem.at[1])

    take(P_U, (0, 2), flip=P_UT)
    products(handed, DP, [(ET, ET, True), (P_UT, P_UT, True)], first=True, tiles=[(top, top)])
    send_sym(from_handed(DP), DP_L, 0, right)
    for q in range(4):
        squares = own_block(ZD, q, squares)
        send(from_own(ZD), Z_R, q, left)
        send(from_own(ZD), Z_U, q, down)
    squares = 2.0 * squares
    trace = jnp.zeros((8, B), F32)
    onsite_load.wait()
    diag = lax.broadcasted_iota(jnp.int32, (B, B), 0) == lax.broadcasted_iota(jnp.int32, (B, B), 1)
    for z, q in ((0, 0), (1, 3)):
        loads[DG, q].wait()
        here = pl.ds(z * B, B)
        raw = own[DG, here, here]
        value = 0.5 * (raw + raw.T) + jnp.where(diag, onsite[z : z + 1, :], 0.0)
        own[DG, here, here] = value
        put_split(DG, here, here, value)
        squares = squares + jnp.sum((value * value).reshape(32, 8, B), axis=0)
        trace = trace + jnp.sum(jnp.where(diag, value, 0.0).reshape(32, 8, B), axis=0)
    loads[DG, 1].wait()
    value = own[DG, top, low] * mask[0, 0].astype(F32)
    own[DG, top, low] = value
    put_split(DG, top, low, value)
    squares = squares + 2.0 * jnp.sum((value * value).reshape(32, 8, B), axis=0)
    flipped = value.T
    own[DG, low, top] = flipped
    put_split(DG, low, top, flipped)
    trace = trace[:, :128] + trace[:, 128:]
    squares = squares[:, :128] + squares[:, 128:]
    part[0, 0:4, :] = trace[0:4] + trace[4:8]
    part[0, 4:8, :] = squares[0:4] + squares[4:8]

    small = []

    def send_part(stage, peers, base):
        copies = []
        for n, peer in enumerate(peers):
            copy = pltpu.make_async_remote_copy(
                src_ref=part.at[stage],
                dst_ref=gath.at[base + n],
                send_sem=ar_send.at[base + n],
                recv_sem=ar_recv.at[base + n],
                device_id=peer,
                device_id_type=MESH,
            )
            copy.start()
            copies.append(copy)
        small.extend(copies)
        return copies

    def add_parts(stage, copies, base):
        total = part[stage]
        for n, copy in enumerate(copies):
            copy.wait_recv()
            total = total + gath[base + n]
        part[stage + 1] = total

    for q in DQUADS:
        send_sym(from_own(DG), D_W, q, up)
        send_sym(from_own(DG), D_R, q, left)

    take(P_U, (1, 3), flip=P_UT)
    products(handed, DP, [(ET, ET, True), (P_UT, P_UT, True)], first=True, tiles=[(full, low)])
    send_sym(from_handed(DP), DP_L, 1, right)
    send_sym(from_handed(DP), DP_L, 3, right)
    heard(round_sem.at[1])
    col_parts = send_part(0, col_peers, 0)

    products(handed, ZP, [(ET, PR, False)], first=True)
    take(M_R, (0, 1), (M_UR, down))
    take(E_W)
    products(handed, ZP, [(sp(M_R), sp(E_W), False)], tiles=[(top, top), (top, low)])
    for q in (0, 1):
        send(from_handed(ZP), ZP_L, q, right)
    products(y, ER, [(DG, ER, False)], first=True)
    products(y, ML, [(DG, ML, False)], first=True)
    take(M_R, (2, 3), (M_UR, down))
    products(handed, ZP, [(sp(M_R), sp(E_W), False)], tiles=[(low, top), (low, low)])
    for q in (2, 3):
        send(from_handed(ZP), ZP_L, q, right)
    products(
        y,
        DG,
        [(DG, DG, False), (ER, ER, True), (ML, ML, True), (ZD, ZD, True), (PR, PR, True)],
        first=True,
        tiles=[(top, top), (full, low)],
    )
    add_parts(0, col_parts, 0)
    row_parts = send_part(1, row_peers, 15)
    take_d(D_W)
    products(handed, QQ, [(ET, ZD, False), (sp(M_R), sp(D_W), False)], first=True)
    take(Z_R, (0,), (Z_UR, down))
    products(
        y,
        ZD,
        [(DG, ZD, False), (ZD, sp(D_W), False), (ER, sp(M_R), False), (PR, sp(E_W), True)],
        first=True,
    )
    take(Z_R, (1,), (Z_UR, down))
    products(handed, QQ, [(sp(Z_R), sp(E_W), True)], tiles=[(top, top), (top, low)])
    for q in (0, 1):
        send(from_handed(QQ), Q_L, q, right)
    take_t(Z_U)
    products(y, ER, [(ZD, sp(M_R), True), (sp(Z_U), sp(P_U), False)])
    take(Z_R, (2,), (Z_UR, down))
    products(y, PR, [(DG, PR, False), (ZD, sp(E_W), False)], first=True)
    take(Z_R, (3,), (Z_UR, down))
    products(handed, QQ, [(sp(Z_R), sp(E_W), True)], tiles=[(low, top), (low, low)])
    for q in (2, 3):
        send(from_handed(QQ), Q_L, q, right)
    take_t(M_UR)
    products(
        y,
        DG,
        [(sp(Z_U), sp(Z_U), True), (sp(M_UR), sp(M_UR), True)],
        tiles=[(top, top), (full, low)],
    )
    add_parts(1, row_parts, 15)
    total = part[2]
    t1 = jnp.sum(total[0:4, :])
    t2 = jnp.sum(total[4:8, :])
    goal = float(nrow * ncol * B)
    lean = (jnp.abs(t2 - goal) - jnp.abs(2.0 * t1 - t2 - goal)) / B
    steer[...] = 2.0 / (1.0 + jnp.exp(-jnp.full((8, B), lean, F32)))
    take_d(D_R, (0,), (D_WR, up))
    products(y, ER, [(PR, sp(Z_R), True)])
    products(y, PR, [(ER, sp(Z_R), False)])
    finish(DG, DP_L)
    finish(ZD, ZP_L)
    take_d(D_R, (1,), (D_WR, up))
    products(y, ER, [(ER, sp(D_R), False)], tiles=[(full, top)])
    take(Z_UR)
    products(y, ER, [(sp(M_UR), sp(Z_UR), False)])
    finish(ER, quads=(0, 2))
    take_d(D_R, (3,), (D_WR, up))
    products(y, ER, [(ER, sp(D_R), False)], tiles=[(full, low)])
    finish(ER, quads=(1, 3))
    finish(ML, Q_L, (0, 1))
    take_d(D_WR, (0, 1))
    products(y, PR, [(PR, sp(D_WR), False)], tiles=[(full, top)])
    finish(PR, quads=(0, 2))
    take_d(D_WR, (3,))
    products(y, PR, [(PR, sp(D_WR), False)], tiles=[(full, low)])
    finish(PR, quads=(1, 3))
    finish(ML, Q_L, (2, 3))

    for copy in small:
        copy.wait_send()
    for copy in sent.values():
        copy.wait_send()


def write(y, out, zero, sem):
    zero[...] = jnp.zeros_like(zero)
    copies = [(z, slot) for z in range(2) for slot in range(14)]
    started = []
    for t in range(5):
        for q in DQUADS if t == DG else range(4):
            z, z2 = QUADS[q]
            slot = (1 if q == 1 else 0) if t == DG else block_slot(t, z, z2)
            copies.remove((z, slot))
            started.append((y.at[t, pl.ds(z * B, B), pl.ds(z2 * B, B)], z, slot))
    started = [
        pltpu.make_async_copy(source, out.at[z, slot], sem.at[z * 14 + slot])
        for source, z, slot in started + [(zero, z, slot) for z, slot in copies]
    ]
    for copy in started:
        copy.start()
    for copy in started:
        copy.wait()


def shards(stored_blocks, onsite, bond_mask):
    squared = pl.pallas_call(
        kernel,
        out_shape=pltpu.VMEM((5, W2, W2), F32),
        in_specs=[
            pl.BlockSpec(memory_space=pltpu.HBM),
            pl.BlockSpec(memory_space=pltpu.HBM),
            pl.BlockSpec(memory_space=pltpu.HBM),
        ],
        out_specs=pl.BlockSpec(memory_space=pltpu.VMEM),
        scratch_shapes=[
            pltpu.VMEM((5, W2, W2), F32),
            pltpu.VMEM((NRX, W2, W2), F32),
            pltpu.VMEM((NSPLIT, W2, W2), BF16),
            pltpu.VMEM((NSPLIT, W2, W2), BF16),
            pltpu.VMEM((3, W2, W2), F32),
            pltpu.VMEM((3, 8, 128), F32),
            pltpu.VMEM((22, 8, 128), F32),
            pltpu.VMEM((8, B), F32),
            pltpu.VMEM((2, B), F32),
            pltpu.SMEM((2, 13), jnp.int32),
            pltpu.SemaphoreType.DMA((21,)),
            pltpu.SemaphoreType.DMA((NRX * 5,)),
            pltpu.SemaphoreType.DMA((NRX * 5,)),
            pltpu.SemaphoreType.DMA((22,)),
            pltpu.SemaphoreType.DMA((22,)),
            pltpu.SemaphoreType.REGULAR((2,)),
        ],
        compiler_params=pltpu.CompilerParams(
            collective_id=0, has_side_effects=True, vmem_limit_bytes=50 * 1024 * 1024
        ),
        name="sp2_step",
    )(stored_blocks[0, 0], onsite[0, 0], bond_mask[0, 0])
    result = pl.pallas_call(
        write,
        out_shape=jax.ShapeDtypeStruct(stored_blocks.shape[2:], F32),
        in_specs=[pl.BlockSpec(memory_space=pltpu.VMEM)],
        out_specs=pl.BlockSpec(memory_space=pltpu.HBM),
        scratch_shapes=[pltpu.VMEM((B, B), F32), pltpu.SemaphoreType.DMA((28,))],
        compiler_params=pltpu.CompilerParams(vmem_limit_bytes=4 * 1024 * 1024),
        name="write_out",
    )(squared)
    return result[None, None]


def solution(mesh):
    in_specs = (
        P("row", "col", None, None, None, None),
        P("row", "col", None, None),
        P("row", "col", None, None),
    )
    out_specs = P("row", "col", None, None, None, None)
    return jax.shard_map(shards, mesh=mesh, in_specs=in_specs, out_specs=out_specs, check_vma=False)
```

time: 83.3 us -> 106 us (1.27)
  Pallas kernels: 83 us -> 105 us
    pallas_call x1, Pallas kernels: 79.8 us -> 102 us  [shards(): pl.pallas_call(kernel, out_shape=pltpu.VMEM((5, W2, W2), F32), in_specs=[...]
where the time goes in v5:
time: 106 us
  Pallas kernels  105 us (99%)
    pallas_call x1, Pallas kernels, shards(): pl.pallas_call(kernel, out_shape=pltpu.VMEM((5, W2, W2), F32), in_specs=[...  102 us
    pallas_call x1, Pallas kernels, shards(): pl.pallas_call(write, out_shape=jax.ShapeDtypeStruct(stored_blocks.shape[...  3.19 us

profile of v5, /device:TPU:0, one launch (start us, length us, event | category | flops | bytes accessed | tf_op | source)
XLA Modules:
  0.0 105.5 jit_solution(13879176251600763227)
XLA Ops:
  0.0 102.2 %sp2_step.1.y = f32[5,512,512]{2,1,0:T(8,128)S(1)} custom-call(f32[2,14,256,256]{3,2,1,0:T(8,128)} %bitcast.4, f32[2,256]{1,0:T(2,128)} %bitcast.5, s32[2,13]{1,0:T(2,128)} %bitcast.6), custom_call_target="tpu_custom_call" | custom-call | tf_op jit(solution)/shard_map/sp2_step/pallas_call | solution.py:439
  102.2 3.2 %write_out.1 = f32[2,14,256,256]{3,2,1,0:T(8,128)} custom-call(f32[5,512,512]{2,1,0:T(8,128)S(1)} %sp2_step.1.y), custom_call_target="tpu_custom_call" | custom-call | tf_op jit(solution)/shard_map/write_out/pallas_call | solution.py:471

commit v6 on v5

--- a/solution.py
+++ b/solution.py
@@ -246,15 +246,16 @@
     send(from_own(ML), M_R, 0, left)
     squares = own_block(PR, 2, squares)
     send(from_own(PR), P_U, 2, down)
-    for p, m in ((1, 1), (3, 2)):
-        squares = own_block(PR, p, squares)
-        send(from_own(PR), P_U, p, down)
-        squares = own_block(ML, m, squares)
-        send(from_own(ML), M_R, m, left)
-    squares = own_block(ML, 3, squares)
+    squares = own_block(PR, 1, squares)
+    send(from_own(PR), P_U, 1, down)
+    squares = own_block(ML, 1, squares)
+    send(from_own(ML), M_R, 1, left)
+    squares = own_block(PR, 3, squares)
+    send(from_own(PR), P_U, 3, down)
+    for q in (2, 3):
+        squares = own_block(ML, q, squares)
     for q in range(4):
         squares = own_block(ER, q, squares)
-    send(from_own(ML), M_R, 3, left)
     for q, (i, j) in enumerate(QUADS):
         send(from_own(ER), E_W, q, up)
         value = own[ER, pl.ds(i * B, B), pl.ds(j * B, B)].T
@@ -267,7 +268,6 @@
     send_sym(from_handed(DP), DP_L, 0, right)
     for q in range(4):
         squares = own_block(ZD, q, squares)
-        send(from_own(ZD), Z_R, q, left)
         send(from_own(ZD), Z_U, q, down)
     squares = 2.0 * squares
     trace = jnp.zeros((8, B), F32)
@@ -320,6 +320,12 @@
             total = total + gath[base + n]
         part[stage + 1] = total
 
+    heard(round_sem.at[1])
+    col_parts = send_part(0, col_peers, 0)
+    for q in (2, 3):
+        send(from_own(ML), M_R, q, left)
+    for q in range(4):
+        send(from_own(ZD), Z_R, q, left)
     for q in DQUADS:
         send_sym(from_own(DG), D_W, q, up)
         send_sym(from_own(DG), D_R, q, left)
@@ -328,8 +334,6 @@
     products(handed, DP, [(ET, ET, True), (P_UT, P_UT, True)], first=True, tiles=[(full, low)])
     send_sym(from_handed(DP), DP_L, 1, right)
     send_sym(from_handed(DP), DP_L, 3, right)
-    heard(round_sem.at[1])
-    col_parts = send_part(0, col_peers, 0)
 
     products(handed, ZP, [(ET, PR, False)], first=True)
     take(M_R, (0, 1), (M_UR, down))

time: 106 us -> 79.7 us (0.75)
  Pallas kernels: 105 us -> 79.5 us
    pallas_call x1, Pallas kernels: 102 us -> 76.3 us  [shards(): pl.pallas_call(kernel, out_shape=pltpu.VMEM((5, W2, W2), F32), in_specs=[...]
where the time goes in v6:
time: 79.7 us; the launch traced here: 79.6 us
  Pallas kernels  79.5 us (100%)
    pallas_call x1, Pallas kernels, shards(): pl.pallas_call(kernel, out_shape=pltpu.VMEM((5, W2, W2), F32), in_specs=[...  76.3 us
    pallas_call x1, Pallas kernels, shards(): pl.pallas_call(write, out_shape=jax.ShapeDtypeStruct(stored_blocks.shape[...  3.19 us

profile of v6, /device:TPU:0, one launch (start us, length us, event | category | flops | bytes accessed | tf_op | source)
XLA Modules:
  0.0 79.6 jit_solution(7875768162925985063)
XLA Ops:
  0.0 76.3 %sp2_step.1.y = f32[5,512,512]{2,1,0:T(8,128)S(1)} custom-call(f32[2,14,256,256]{3,2,1,0:T(8,128)} %bitcast.4, f32[2,256]{1,0:T(2,128)} %bitcast.5, s32[2,13]{1,0:T(2,128)} %bitcast.6), custom_call_target="tpu_custom_call" | custom-call | tf_op jit(solution)/shard_map/sp2_step/pallas_call | solution.py:443
  76.3 3.2 %write_out.1 = f32[2,14,256,256]{3,2,1,0:T(8,128)} custom-call(f32[5,512,512]{2,1,0:T(8,128)S(1)} %sp2_step.1.y), custom_call_target="tpu_custom_call" | custom-call | tf_op jit(solution)/shard_map/write_out/pallas_call | solution.py:475

commit v7 on v6

--- a/solution.py
+++ b/solution.py
@@ -68,9 +68,7 @@
     mask_load = pltpu.make_async_copy(mask_in, mask, in_sem.at[19])
     mask_load.start()
     loads = {}
-    for t, q in [(t, q) for q in range(4) for t in (PR, ML)] + [
-        (t, q) for t in (ER, ZD) for q in range(4)
-    ]:
+    for t, q in [(t, q) for q in (0, 2, 1, 3) for t in (PR, ML, ER)] + [(ZD, q) for q in range(4)]:
         z, z2 = QUADS[q]
         loads[t, q] = pltpu.make_async_copy(
             stored.at[z, block_slot(t, z, z2)],
@@ -96,7 +94,7 @@
 
     sent = {}
 
-    def send_piece(source, rxi, p, where, peer):
+    def send_piece(source, rxi, p, where, peer, start=True):
         copy = pltpu.make_async_remote_copy(
             src_ref=source(*where),
             dst_ref=rx.at[(rxi,) + where],
@@ -105,16 +103,17 @@
             device_id=peer,
             device_id_type=MESH,
         )
-        copy.start()
+        if start:
+            copy.start()
         sent[rxi, p] = copy
 
     def send(source, rxi, q, peer):
         i, j = QUADS[q]
         send_piece(source, rxi, q, (pl.ds(i * B, B), pl.ds(j * B, B)), peer)
 
-    def send_sym(source, rxi, q, peer):
+    def send_sym(source, rxi, q, peer, start=True):
         for p, r, nr, c, nc in SYM[q]:
-            send_piece(source, rxi, p, (pl.ds(r, nr), pl.ds(c, nc)), peer)
+            send_piece(source, rxi, p, (pl.ds(r, nr), pl.ds(c, nc)), peer, start)
 
     def arrive_sym(rxi, q, forward=None):
         for p, r, nr, c, nc in SYM[q]:
@@ -148,7 +147,7 @@
             put_split(t, rows, cols, value)
             return total + jnp.sum((value * value).reshape(8, 8, B), axis=0)
 
-        return lax.fori_loop(0, 4, strip_step, squares)
+        return lax.fori_loop(0, 4, strip_step, squares, unroll=True)
 
     def prep(rxi, q, flip=None, keep=True):
         i, j = QUADS[q]
@@ -235,37 +234,64 @@
                 y[yi, rows, cols] = value
                 return carry
 
-            lax.fori_loop(0, 4, strip_step, 0)
+            lax.fori_loop(0, 4, strip_step, 0, unroll=True)
 
     top, low = pl.ds(0, B), pl.ds(B, B)
+    def turn_own(quads):
+        for q in quads:
+            i, j = QUADS[q]
+            value = own[ER, pl.ds(i * B, B), pl.ds(j * B, B)].T
+            put_split(ET, pl.ds(j * B, B), pl.ds(i * B, B), value)
+
     squares = own_block(PR, 0, jnp.zeros((8, B), F32))
     heard(barrier)
     send(from_own(PR), P_U, 0, down)
     tell(round_sem.at[0])
     squares = own_block(ML, 0, squares)
     send(from_own(ML), M_R, 0, left)
+    squares = own_block(ER, 0, squares)
+    send(from_own(ER), E_W, 0, up)
     squares = own_block(PR, 2, squares)
     send(from_own(PR), P_U, 2, down)
+    squares = own_block(ER, 2, squares)
+    send(from_own(ER), E_W, 2, up)
+    turn_own((0, 2))
     squares = own_block(PR, 1, squares)
     send(from_own(PR), P_U, 1, down)
+    send_sym(from_handed(DP), DP_L, 0, right, start=False)
+    diagonal_sums = [(ET, ET, True), (P_UT, P_UT, True)]
+
+    def start_of_diagonal():
+        take(P_U, (0, 2), flip=P_UT)
+        products(handed, DP, diagonal_sums, first=True, tiles=[(top, top)])
+        for p in (0, 1):
+            sent[DP_L, p].start()
+
+    pl.when(lax.rem(row, 2) == 1)(start_of_diagonal)
+    squares = own_block(PR, 3, squares)
+    send(from_own(PR), P_U, 3, down)
+    for q in (1, 3):
+        squares = own_block(ER, q, squares)
+        send(from_own(ER), E_W, q, up)
     squares = own_block(ML, 1, squares)
     send(from_own(ML), M_R, 1, left)
-    squares = own_block(PR, 3, squares)
-    send(from_own(PR), P_U, 3, down)
+    heard(round_sem.at[0])
+    tell(round_sem.at[1])
+    pl.when(lax.rem(row, 2) == 0)(start_of_diagonal)
+    turn_own((1, 3))
+    for q in (1, 3):
+        send_sym(from_handed(DP), DP_L, q, right, start=False)
+
+    def rest_of_diagonal():
+        take(P_U, (1, 3), flip=P_UT)
+        products(handed, DP, diagonal_sums, first=True, tiles=[(full, low)])
+        for p in (2, 3, 4):
+            sent[DP_L, p].start()
+
+    pl.when(lax.rem(row, 2) == 1)(rest_of_diagonal)
     for q in (2, 3):
         squares = own_block(ML, q, squares)
-    for q in range(4):
-        squares = own_block(ER, q, squares)
-    for q, (i, j) in enumerate(QUADS):
-        send(from_own(ER), E_W, q, up)
-        value = own[ER, pl.ds(i * B, B), pl.ds(j * B, B)].T
-        put_split(ET, pl.ds(j * B, B), pl.ds(i * B, B), value)
-    heard(round_sem.at[0])
-    tell(round_sem.at[1])
-
-    take(P_U, (0, 2), flip=P_UT)
-    products(handed, DP, [(ET, ET, True), (P_UT, P_UT, True)], first=True, tiles=[(top, top)])
-    send_sym(from_handed(DP), DP_L, 0, right)
+    send(from_own(ML), M_R, 2, left)
     for q in range(4):
         squares = own_block(ZD, q, squares)
         send(from_own(ZD), Z_U, q, down)
@@ -292,8 +318,8 @@
     put_split(DG, low, top, flipped)
     trace = trace[:, :128] + trace[:, 128:]
     squares = squares[:, :128] + squares[:, 128:]
-    part[0, 0:4, :] = trace[0:4] + trace[4:8]
-    part[0, 4:8, :] = squares[0:4] + squares[4:8]
+    part[0, 0:1, :] = jnp.sum(trace, axis=0, keepdims=True)
+    part[0, 1:2, :] = jnp.sum(squares, axis=0, keepdims=True)
 
     small = []
 
@@ -322,22 +348,18 @@
 
     heard(round_sem.at[1])
     col_parts = send_part(0, col_peers, 0)
-    for q in (2, 3):
-        send(from_own(ML), M_R, q, left)
+    send(from_own(ML), M_R, 3, left)
     for q in range(4):
         send(from_own(ZD), Z_R, q, left)
     for q in DQUADS:
         send_sym(from_own(DG), D_W, q, up)
         send_sym(from_own(DG), D_R, q, left)
 
-    take(P_U, (1, 3), flip=P_UT)
-    products(handed, DP, [(ET, ET, True), (P_UT, P_UT, True)], first=True, tiles=[(full, low)])
-    send_sym(from_handed(DP), DP_L, 1, right)
-    send_sym(from_handed(DP), DP_L, 3, right)
+    pl.when(lax.rem(row, 2) == 0)(rest_of_diagonal)
 
     products(handed, ZP, [(ET, PR, False)], first=True)
     take(M_R, (0, 1), (M_UR, down))
-    take(E_W)
+    take(E_W, (0, 2, 1, 3))
     products(handed, ZP, [(sp(M_R), sp(E_W), False)], tiles=[(top, top), (top, low)])
     for q in (0, 1):
         send(from_handed(ZP), ZP_L, q, right)
@@ -358,21 +380,20 @@
     row_parts = send_part(1, row_peers, 15)
     take_d(D_W)
     products(handed, QQ, [(ET, ZD, False), (sp(M_R), sp(D_W), False)], first=True)
-    take(Z_R, (0,), (Z_UR, down))
+    products(y, PR, [(DG, PR, False), (ZD, sp(E_W), False)], first=True)
+    take(Z_R, (0, 1), (Z_UR, down))
+    products(handed, QQ, [(sp(Z_R), sp(E_W), True)], tiles=[(top, top), (top, low)])
+    for q in (0, 1):
+        send(from_handed(QQ), Q_L, q, right)
     products(
         y,
         ZD,
         [(DG, ZD, False), (ZD, sp(D_W), False), (ER, sp(M_R), False), (PR, sp(E_W), True)],
         first=True,
     )
-    take(Z_R, (1,), (Z_UR, down))
-    products(handed, QQ, [(sp(Z_R), sp(E_W), True)], tiles=[(top, top), (top, low)])
-    for q in (0, 1):
-        send(from_handed(QQ), Q_L, q, right)
+    take(Z_R, (2,), (Z_UR, down))
     take_t(Z_U)
     products(y, ER, [(ZD, sp(M_R), True), (sp(Z_U), sp(P_U), False)])
-    take(Z_R, (2,), (Z_UR, down))
-    products(y, PR, [(DG, PR, False), (ZD, sp(E_W), False)], first=True)
     take(Z_R, (3,), (Z_UR, down))
     products(handed, QQ, [(sp(Z_R), sp(E_W), True)], tiles=[(low, top), (low, low)])
     for q in (2, 3):
@@ -386,8 +407,8 @@
     )
     add_parts(1, row_parts, 15)
     total = part[2]
-    t1 = jnp.sum(total[0:4, :])
-    t2 = jnp.sum(total[4:8, :])
+    t1 = jnp.sum(total[0:1, :])
+    t2 = jnp.sum(total[1:2, :])
     goal = float(nrow * ncol * B)
     lean = (jnp.abs(t2 - goal) - jnp.abs(2.0 * t1 - t2 - goal)) / B
     steer[...] = 2.0 / (1.0 + jnp.exp(-jnp.full((8, B), lean, F32)))
@@ -408,10 +429,11 @@
     take_d(D_WR, (0, 1))
     products(y, PR, [(PR, sp(D_WR), False)], tiles=[(full, top)])
     finish(PR, quads=(0, 2))
+    finish(ML, Q_L, (2,))
     take_d(D_WR, (3,))
     products(y, PR, [(PR, sp(D_WR), False)], tiles=[(full, low)])
     finish(PR, quads=(1, 3))
-    finish(ML, Q_L, (2, 3))
+    finish(ML, Q_L, (3,))
 
     for copy in small:
         copy.wait_send()
@@ -455,8 +477,8 @@
             pltpu.VMEM((NSPLIT, W2, W2), BF16),
             pltpu.VMEM((NSPLIT, W2, W2), BF16),
             pltpu.VMEM((3, W2, W2), F32),
-            pltpu.VMEM((3, 8, 128), F32),
-            pltpu.VMEM((22, 8, 128), F32),
+            pltpu.VMEM((3, 2, 128), F32),
+            pltpu.VMEM((22, 2, 128), F32),
             pltpu.VMEM((8, B), F32),
             pltpu.VMEM((2, B), F32),
             pltpu.SMEM((2, 13), jnp.int32),

time: 79.7 us -> 78.9 us (0.990)
  Pallas kernels: 79.5 us -> 78.7 us
    pallas_call x1, Pallas kernels: 76.3 us -> 75.5 us  [shards(): pl.pallas_call(kernel, out_shape=pltpu.VMEM((5, W2, W2), F32), in_specs=[...]
where the time goes in v7:
time: 78.9 us; the launch traced here: 78.8 us
  Pallas kernels  78.7 us (100%)
    pallas_call x1, Pallas kernels, shards(): pl.pallas_call(kernel, out_shape=pltpu.VMEM((5, W2, W2), F32), in_specs=[...  75.5 us
    pallas_call x1, Pallas kernels, shards(): pl.pallas_call(write, out_shape=jax.ShapeDtypeStruct(stored_blocks.shape[...  3.19 us

profile of v7, /device:TPU:0, one launch (start us, length us, event | category | flops | bytes accessed | tf_op | source)
XLA Modules:
  0.0 78.8 jit_solution(6612678136277549974)
XLA Ops:
  0.0 75.5 %sp2_step.1.y = f32[5,512,512]{2,1,0:T(8,128)S(1)} custom-call(f32[2,14,256,256]{3,2,1,0:T(8,128)} %bitcast.4, f32[2,256]{1,0:T(2,128)} %bitcast.5, s32[2,13]{1,0:T(2,128)} %bitcast.6), custom_call_target="tpu_custom_call" | custom-call | tf_op jit(solution)/shard_map/sp2_step/pallas_call | solution.py:465
  75.5 3.2 %write_out.1 = f32[2,14,256,256]{3,2,1,0:T(8,128)} custom-call(f32[5,512,512]{2,1,0:T(8,128)S(1)} %sp2_step.1.y), custom_call_target="tpu_custom_call" | custom-call | tf_op jit(solution)/shard_map/write_out/pallas_call | solution.py:497

commit v8 on v7

--- a/solution.py
+++ b/solution.py
@@ -107,9 +107,9 @@
             copy.start()
         sent[rxi, p] = copy
 
-    def send(source, rxi, q, peer):
+    def send(source, rxi, q, peer, start=True):
         i, j = QUADS[q]
-        send_piece(source, rxi, q, (pl.ds(i * B, B), pl.ds(j * B, B)), peer)
+        send_piece(source, rxi, q, (pl.ds(i * B, B), pl.ds(j * B, B)), peer, start)
 
     def send_sym(source, rxi, q, peer, start=True):
         for p, r, nr, c, nc in SYM[q]:
@@ -248,13 +248,24 @@
     send(from_own(PR), P_U, 0, down)
     tell(round_sem.at[0])
     squares = own_block(ML, 0, squares)
-    send(from_own(ML), M_R, 0, left)
+    for q in (0, 1):
+        send(from_own(ML), M_R, q, left, start=False)
+
+    def start_m(*quads):
+        for q in quads:
+            sent[M_R, q].start()
+
+    odd = lax.rem(row, 2) == 1
+    even = lax.rem(row, 2) == 0
+    pl.when(odd)(lambda: start_m(0))
     squares = own_block(ER, 0, squares)
     send(from_own(ER), E_W, 0, up)
     squares = own_block(PR, 2, squares)
     send(from_own(PR), P_U, 2, down)
     squares = own_block(ER, 2, squares)
     send(from_own(ER), E_W, 2, up)
+    squares = own_block(ML, 1, squares)
+    pl.when(odd)(lambda: start_m(1))
     turn_own((0, 2))
     squares = own_block(PR, 1, squares)
     send(from_own(PR), P_U, 1, down)
@@ -267,17 +278,16 @@
         for p in (0, 1):
             sent[DP_L, p].start()
 
-    pl.when(lax.rem(row, 2) == 1)(start_of_diagonal)
+    pl.when(odd)(start_of_diagonal)
     squares = own_block(PR, 3, squares)
     send(from_own(PR), P_U, 3, down)
     for q in (1, 3):
         squares = own_block(ER, q, squares)
         send(from_own(ER), E_W, q, up)
-    squares = own_block(ML, 1, squares)
-    send(from_own(ML), M_R, 1, left)
+    pl.when(even)(lambda: start_m(0, 1))
     heard(round_sem.at[0])
     tell(round_sem.at[1])
-    pl.when(lax.rem(row, 2) == 0)(start_of_diagonal)
+    pl.when(even)(start_of_diagonal)
     turn_own((1, 3))
     for q in (1, 3):
         send_sym(from_handed(DP), DP_L, q, right, start=False)
@@ -288,7 +298,7 @@
         for p in (2, 3, 4):
             sent[DP_L, p].start()
 
-    pl.when(lax.rem(row, 2) == 1)(rest_of_diagonal)
+    pl.when(odd)(rest_of_diagonal)
     for q in (2, 3):
         squares = own_block(ML, q, squares)
     send(from_own(ML), M_R, 2, left)
@@ -355,19 +365,19 @@
         send_sym(from_own(DG), D_W, q, up)
         send_sym(from_own(DG), D_R, q, left)
 
-    pl.when(lax.rem(row, 2) == 0)(rest_of_diagonal)
-
     products(handed, ZP, [(ET, PR, False)], first=True)
+    pl.when(even)(rest_of_diagonal)
+
     take(M_R, (0, 1), (M_UR, down))
-    take(E_W, (0, 2, 1, 3))
-    products(handed, ZP, [(sp(M_R), sp(E_W), False)], tiles=[(top, top), (top, low)])
-    for q in (0, 1):
+    for q, quads, cols in ((0, (0, 2), top), (1, (1, 3), low)):
+        take(E_W, quads)
+        products(handed, ZP, [(sp(M_R), sp(E_W), False)], tiles=[(top, cols)])
         send(from_handed(ZP), ZP_L, q, right)
     products(y, ER, [(DG, ER, False)], first=True)
     products(y, ML, [(DG, ML, False)], first=True)
     take(M_R, (2, 3), (M_UR, down))
-    products(handed, ZP, [(sp(M_R), sp(E_W), False)], tiles=[(low, top), (low, low)])
-    for q in (2, 3):
+    for q, cols in ((2, top), (3, low)):
+        products(handed, ZP, [(sp(M_R), sp(E_W), False)], tiles=[(low, cols)])
         send(from_handed(ZP), ZP_L, q, right)
     products(
         y,
@@ -382,8 +392,8 @@
     products(handed, QQ, [(ET, ZD, False), (sp(M_R), sp(D_W), False)], first=True)
     products(y, PR, [(DG, PR, False), (ZD, sp(E_W), False)], first=True)
     take(Z_R, (0, 1), (Z_UR, down))
-    products(handed, QQ, [(sp(Z_R), sp(E_W), True)], tiles=[(top, top), (top, low)])
-    for q in (0, 1):
+    for q, cols in ((0, top), (1, low)):
+        products(handed, QQ, [(sp(Z_R), sp(E_W), True)], tiles=[(top, cols)])
         send(from_handed(QQ), Q_L, q, right)
     products(
         y,
@@ -395,8 +405,8 @@
     take_t(Z_U)
     products(y, ER, [(ZD, sp(M_R), True), (sp(Z_U), sp(P_U), False)])
     take(Z_R, (3,), (Z_UR, down))
-    products(handed, QQ, [(sp(Z_R), sp(E_W), True)], tiles=[(low, top), (low, low)])
-    for q in (2, 3):
+    for q, cols in ((2, top), (3, low)):
+        products(handed, QQ, [(sp(Z_R), sp(E_W), True)], tiles=[(low, cols)])
         send(from_handed(QQ), Q_L, q, right)
     take_t(M_UR)
     products(

time: 78.9 us -> 77.8 us (0.986)
  Pallas kernels: 78.7 us -> 77.3 us
    pallas_call x1, Pallas kernels: 75.5 us -> 74.1 us  [shards(): pl.pallas_call(kernel, out_shape=pltpu.VMEM((5, W2, W2), F32), in_specs=[...]
where the time goes in v8:
time: 77.8 us; the launch traced here: 77.5 us
  Pallas kernels  77.3 us (99%)
    pallas_call x1, Pallas kernels, shards(): pl.pallas_call(kernel, out_shape=pltpu.VMEM((5, W2, W2), F32), in_specs=[...  74.1 us
    pallas_call x1, Pallas kernels, shards(): pl.pallas_call(write, out_shape=jax.ShapeDtypeStruct(stored_blocks.shape[...  3.19 us

profile of v8, /device:TPU:0, one launch (start us, length us, event | category | flops | bytes accessed | tf_op | source)
XLA Modules:
  0.0 77.5 jit_solution(3805599286803388130)
XLA Ops:
  0.0 74.1 %sp2_step.1.y = f32[5,512,512]{2,1,0:T(8,128)S(1)} custom-call(f32[2,14,256,256]{3,2,1,0:T(8,128)} %bitcast.4, f32[2,256]{1,0:T(2,128)} %bitcast.5, s32[2,13]{1,0:T(2,128)} %bitcast.6), custom_call_target="tpu_custom_call" | custom-call | tf_op jit(solution)/shard_map/sp2_step/pallas_call | solution.py:475
  74.1 3.2 %write_out.1 = f32[2,14,256,256]{3,2,1,0:T(8,128)} custom-call(f32[5,512,512]{2,1,0:T(8,128)S(1)} %sp2_step.1.y), custom_call_target="tpu_custom_call" | custom-call | tf_op jit(solution)/shard_map/write_out/pallas_call | solution.py:507

commit v9 on v8

--- a/solution.py
+++ b/solution.py
@@ -298,10 +298,29 @@
         for p in (2, 3, 4):
             sent[DP_L, p].start()
 
+    def own_zp():
+        products(handed, ZP, [(ET, PR, False)], first=True)
+
+    for q in (0, 1):
+        send(from_rx(M_R), M_UR, q, down, start=False)
+        send(from_handed(ZP), ZP_L, q, right, start=False)
+
+    def top_of_zp():
+        for q in (0, 1):
+            sent[M_R, q].wait_recv()
+            sent[M_UR, q].start()
+            prep(M_R, q)
+        for q, quads, cols in ((0, (0, 2), top), (1, (1, 3), low)):
+            take(E_W, quads)
+            products(handed, ZP, [(sp(M_R), sp(E_W), False)], tiles=[(top, cols)])
+            sent[ZP_L, q].start()
+
     pl.when(odd)(rest_of_diagonal)
-    for q in (2, 3):
-        squares = own_block(ML, q, squares)
+    squares = own_block(ML, 2, squares)
     send(from_own(ML), M_R, 2, left)
+    pl.when(odd)(own_zp)
+    pl.when(odd)(top_of_zp)
+    squares = own_block(ML, 3, squares)
     for q in range(4):
         squares = own_block(ZD, q, squares)
         send(from_own(ZD), Z_U, q, down)
@@ -365,14 +384,9 @@
         send_sym(from_own(DG), D_W, q, up)
         send_sym(from_own(DG), D_R, q, left)
 
-    products(handed, ZP, [(ET, PR, False)], first=True)
+    pl.when(even)(own_zp)
     pl.when(even)(rest_of_diagonal)
-
-    take(M_R, (0, 1), (M_UR, down))
-    for q, quads, cols in ((0, (0, 2), top), (1, (1, 3), low)):
-        take(E_W, quads)
-        products(handed, ZP, [(sp(M_R), sp(E_W), False)], tiles=[(top, cols)])
-        send(from_handed(ZP), ZP_L, q, right)
+    pl.when(even)(top_of_zp)
     products(y, ER, [(DG, ER, False)], first=True)
     products(y, ML, [(DG, ML, False)], first=True)
     take(M_R, (2, 3), (M_UR, down))

time: 77.8 us -> 77.5 us (level)
  no operation moved by 1% of the time
where the time goes in v9:
time: 77.5 us; the launch traced here: 77.4 us
  Pallas kernels  77.3 us (100%)
    pallas_call x1, Pallas kernels, shards(): pl.pallas_call(kernel, out_shape=pltpu.VMEM((5, W2, W2), F32), in_specs=[...  74.1 us
    pallas_call x1, Pallas kernels, shards(): pl.pallas_call(write, out_shape=jax.ShapeDtypeStruct(stored_blocks.shape[...  3.19 us

profile of v9, /device:TPU:0, one launch (start us, length us, event | category | flops | bytes accessed | tf_op | source)
XLA Modules:
  0.0 77.4 jit_solution(4212619819007304548)
XLA Ops:
  0.0 74.1 %sp2_step.1.y = f32[5,512,512]{2,1,0:T(8,128)S(1)} custom-call(f32[2,14,256,256]{3,2,1,0:T(8,128)} %bitcast.4, f32[2,256]{1,0:T(2,128)} %bitcast.5, s32[2,13]{1,0:T(2,128)} %bitcast.6), custom_call_target="tpu_custom_call" | custom-call | tf_op jit(solution)/shard_map/sp2_step/pallas_call | solution.py:489
  74.1 3.2 %write_out.1 = f32[2,14,256,256]{3,2,1,0:T(8,128)} custom-call(f32[5,512,512]{2,1,0:T(8,128)S(1)} %sp2_step.1.y), custom_call_target="tpu_custom_call" | custom-call | tf_op jit(solution)/shard_map/write_out/pallas_call | solution.py:521
